TPU v7x, 1024 devices: a whole 4x8x16 slice. The times are simulated.
1024 devices in a mesh: ctx: 32 (over z_hi, x, core), ch: 32 (over z_lo, y).
Axes of the slice: x: 4, y: 8, z: 16 (z_hi: 4, z_lo: 4; z = z_hi * 4 + z_lo), core: 2. Of those that a mesh axis runs over, the one named last changes fastest.
Arguments:
- value_in: bfloat16 [8192, 16384], P('ch', 'ctx'), may hold values from -6 to 6
- key_in: bfloat16 [8192, 16384], P('ch', 'ctx'), may hold values from -6 to 6
- gate_first: bfloat16 [8192, 16384], P('ch', 'ctx'), may hold values from -6 to 6
- gate_second: bfloat16 [8192, 16384], P('ch', 'ctx'), may hold values from -6 to 6
- gate_long: bfloat16 [8192, 16384], P('ch', 'ctx'), may hold values from -6 to 6
- filter_first: bfloat16 [512, 128], P('ch'), may hold values from -0.5 to 0.5
- filter_second: bfloat16 [512, 128], P('ch'), may hold values from -0.5 to 0.5
- long_filter: bfloat16 [8192, 16384], P(('ch', 'ctx')), may hold values from -0.046875 to 0.046875
- skip_gain: float32 [8192], P('ch'), may hold values from 0.5 to 1.5
Outputs:
- mixed_out: bfloat16 [8192, 16384], P('ch', 'ctx')
All inputs are finite; a program needn't handle non-finite values.
Results may differ from a plain program's by a relative error of at most 0.0085.
Values may be sent and summed in bfloat16 or wider, within the bound.
No kernel may reach another device: no remote copies, remote signals or barrier semaphores. Data moves between devices by JAX's collectives and lax.ppermute only.
A program may use at most 32 MiB of HBM per device.

v0:
```python
import math

import jax
import jax.numpy as jnp
from jax import lax
from jax.sharding import PartitionSpec as P

HIGH = lax.Precision.HIGH


def from_behind(shard, axis, by):
    devices = lax.axis_size(axis)
    pairs = [(i, i + by) for i in range(devices) if 0 <= i + by < devices]
    return lax.ppermute(shard, axis, pairs)


def band_matrix(filters, tap_count):
    group_count = filters.shape[0]
    zero_one = jnp.zeros((group_count, 1), filters.dtype)
    zero_rest = jnp.zeros((group_count, tap_count), filters.dtype)
    pattern = jnp.concatenate([zero_one, jnp.flip(filters, axis=1), zero_rest], axis=1)
    tiled = jnp.tile(pattern, (1, tap_count))
    return tiled[:, : tap_count * 2 * tap_count].reshape(group_count, tap_count, 2 * tap_count)


def toeplitz_conv(extended, filters, tap_count):
    channels, total_len = extended.shape
    length = total_len - tap_count
    block_count = length // tap_count
    front_half = extended[:, :length].reshape(channels, block_count, tap_count)
    back_half = extended[:, tap_count:].reshape(channels, block_count, tap_count)
    windows = jnp.concatenate([front_half, back_half], axis=2)
    group_count = filters.shape[0]
    windows = windows.reshape(group_count, channels // group_count, block_count, 2 * tap_count)
    toeplitz = band_matrix(filters, tap_count)
    result = jnp.einsum("gts,gcbs->gcbt", toeplitz, windows, preferred_element_type=jnp.float32)
    return result.reshape(channels, length)


def previous_rim(tail):
    return from_behind(tail, "ctx", 1)


def to_channels(data):
    return lax.all_to_all(data, "ctx", split_axis=0, concat_axis=1, tiled=True)


def first_section(mixed_in, gate_first, filter_first, tap_count):
    length = mixed_in.shape[1]
    extended = jnp.concatenate([previous_rim(mixed_in[:, length - tap_count :]), mixed_in], axis=1)
    return (
        gate_first.astype(jnp.float32) * toeplitz_conv(extended, filter_first, tap_count)
    ).astype(jnp.bfloat16)


def dft_tables(size):
    index = jnp.arange(size, dtype=jnp.int32)
    angle = (index[:, None] * index[None, :] % size).astype(jnp.float32) * (-2.0 * math.pi / size)
    return (jnp.cos(angle), jnp.sin(angle))


def split_factor(padded_len):
    outer = 2
    cand = 2
    while cand * cand <= padded_len:
        if padded_len % cand == 0:
            outer = cand
        cand = cand + 2
    return outer


def long_convolution(signal, filt_vals, skip_part):
    channels, length = signal.shape
    padded_len = 2 * length
    rows_outer = split_factor(padded_len)
    rows_inner = padded_len // rows_outer
    half_rows = rows_outer // 2
    outer_cos, outer_sin = dft_tables(rows_outer)
    inner_cos, inner_sin = dft_tables(rows_inner)
    k_index = jnp.arange(rows_outer, dtype=jnp.int32)[:, None]
    n_index = jnp.arange(rows_inner, dtype=jnp.int32)[None, :]
    twid_angle = (k_index * n_index % padded_len).astype(jnp.float32) * (
        -2.0 * math.pi / padded_len
    )
    twid_cos = jnp.cos(twid_angle)
    twid_sin = jnp.sin(twid_angle)
    outer_table = jnp.concatenate([outer_cos[:, :half_rows], outer_sin[:, :half_rows]], axis=0)
    inner_fwd = jnp.concatenate(
        [
            jnp.concatenate([inner_cos, inner_sin], axis=1),
            jnp.concatenate([-inner_sin, inner_cos], axis=1),
        ],
        axis=0,
    )
    inner_back = jnp.concatenate(
        [
            jnp.concatenate([inner_cos, -inner_sin], axis=1),
            jnp.concatenate([inner_sin, inner_cos], axis=1),
        ],
        axis=0,
    )

    def forward(values):
        grid = values.reshape(channels, half_rows, rows_inner)
        parts = jnp.einsum("kn,cnm->ckm", outer_table, grid, precision=HIGH)
        part_re = parts[:, :rows_outer]
        part_im = parts[:, rows_outer:]
        turned_re = part_re * twid_cos - part_im * twid_sin
        turned_im = part_re * twid_sin + part_im * twid_cos
        turned = jnp.concatenate([turned_re, turned_im], axis=2)
        spectrum = jnp.einsum("ckn,nm->ckm", turned, inner_fwd, precision=HIGH)
        return (spectrum[:, :, :rows_inner], spectrum[:, :, rows_inner:])

    sig_re, sig_im = forward(signal)
    filt_re, filt_im = forward(filt_vals)
    prod_re = sig_re * filt_re - sig_im * filt_im
    prod_im = sig_re * filt_im + sig_im * filt_re
    stacked = jnp.concatenate([prod_re, prod_im], axis=2)
    back = jnp.einsum("ckm,mn->ckn", stacked, inner_back, precision=HIGH)
    back_re = back[:, :, :rows_inner]
    back_im = back[:, :, rows_inner:]
    reverted_re = back_re * twid_cos + back_im * twid_sin
    reverted_im = back_im * twid_cos - back_re * twid_sin
    reverted = jnp.concatenate([reverted_re, reverted_im], axis=1)
    result = jnp.einsum("kn,ckm->cnm", outer_table, reverted, precision=HIGH)
    result = result.reshape(channels, length) / padded_len
    return skip_part[:, None] * signal + result


def shards(
    value_in,
    key_in,
    gate_first,
    gate_second,
    gate_long,
    filter_first,
    filter_second,
    long_filter,
    skip_gain,
):
    tap_count = filter_first.shape[1]
    channels, length = value_in.shape
    per_device = channels // lax.axis_size("ctx")
    channel_base = lax.axis_index("ctx") * per_device
    mixed_in = (key_in.astype(jnp.float32) * value_in.astype(jnp.float32)).astype(jnp.bfloat16)
    first_out = first_section(mixed_in, gate_first, filter_first, tap_count)
    prior_first = from_behind(first_out[:, length - tap_count :], "ctx", 1)
    first_wide = jnp.concatenate([prior_first, first_out], axis=1)
    second_out = (
        gate_second.astype(jnp.float32) * toeplitz_conv(first_wide, filter_second, tap_count)
    ).astype(jnp.bfloat16)
    moved = to_channels(second_out)
    skip_here = lax.dynamic_slice_in_dim(skip_gain, channel_base, per_device, 0)
    filt_vals = long_filter.astype(jnp.float32)
    long_out = long_convolution(moved.astype(jnp.float32), filt_vals, skip_here).astype(
        jnp.bfloat16
    )
    back_home = lax.all_to_all(long_out, "ctx", split_axis=1, concat_axis=0, tiled=True)
    return (gate_long.astype(jnp.float32) * back_home.astype(jnp.float32)).astype(jnp.bfloat16)


def solution(mesh):
    placed = (
        P("ch", "ctx"),
        P("ch", "ctx"),
        P("ch", "ctx"),
        P("ch", "ctx"),
        P("ch", "ctx"),
        P("ch", None),
        P("ch", None),
        P(("ch", "ctx"), None),
        P("ch"),
    )
    return jax.shard_map(
        shards, mesh=mesh, in_specs=placed, out_specs=P("ch", "ctx"), check_vma=False
    )
```

profile of v0, /device:TPU:10, one launch (start us, length us, event | category | flops | bytes accessed | tf_op | source)
XLA Modules:
  0.0 109.8 jit_solution(6956796556785582233)
XLA Ops:
  0.0 1.1 %multiply_convert_fusion = bf16[256,512]{1,0:T(8,128)(2,1)S(1)} fusion(bf16[256,512]{1,0:T(8,128)(2,1)} %param.9, bf16[256,512]{1,0:T(8,128)(2,1)} %param.10), kind=kLoop, calls=%fused_computation.56 | loop fusion | flops 524288 | bytes 786432 | tf_op jit(solution)/shard_map/convert_element_type | solution.py:145
  1.2 1.9 %collective-permute-start = (bf16[256,128]{1,0:T(8,128)(2,1)S(1)}, bf16[256,128]{1,0:T(8,128)(2,1)S(1)}, u32[]{:S(2)}, u32[]{:S(2)}) collective-permute-start(bf16[256,128]{1,0:T(8,128)(2,1)S(1)} %slice.72), channel_id=1, source_target_pairs={{0,32},{32,64},{64,96},{96,128},{128,160},{160,192},{192,224},{224... | collective-permute-start | bytes 196616 | tf_op jit(solution)/shard_map/ppermute | solution.py:14
  3.1 0.8 rev.7
  3.9 0.8 rev.8
  4.6 0.1 pad.27.clone
  4.7 0.1 maximum_maximum_fusion
  4.9 0.1 tile.8
  5.1 1.8 %tile.9 = bf16[16,32896]{1,0:T(8,128)(2,1)S(1)} reshape(bf16[16,128,257]{2,1,0:T(8,128)(2,1)S(1)} %tile.8) | data formatting | bytes 2105344 | tf_op jit(solution)/shard_map/tile | solution.py:22
  6.9 0.1 slice.73
  7.0 0.2 copy.52
  7.4 0.5 fusion.31
  7.9 0.2 copy.34
  8.1 0.1 copy-done.7
  8.2 0.1 fusion.36
  8.3 3.5 %collective-permute-start.1 = (bf16[256,128]{1,0:T(8,128)(2,1)S(1)}, bf16[256,128]{1,0:T(8,128)(2,1)S(1)}, u32[]{:S(2)}, u32[]{:S(2)}) collective-permute-start(bf16[256,128]{1,0:T(8,128)(2,1)S(1)} %slice.74), channel_id=1, source_target_pairs={{0,32},{32,64},{64,96},{96,128},{128,160},{160,192},{192,224},{224... | collective-permute-start | bytes 196616 | tf_op jit(solution)/shard_map/ppermute | solution.py:14
  11.8 0.1 tile.20
  12.0 1.8 %tile.21 = bf16[16,32896]{1,0:T(8,128)(2,1)S(1)} reshape(bf16[16,128,257]{2,1,0:T(8,128)(2,1)S(1)} %tile.20) | data formatting | bytes 2105344 | tf_op jit(solution)/shard_map/tile | solution.py:22
  13.8 0.1 slice.75
  13.9 0.2 copy.54
  14.3 0.1 concatenate.67
  14.5 0.5 fusion.29
  14.9 0.2 copy.37
  15.2 0.1 copy-done.8
  15.3 0.8 fusion.48
  16.1 31.0 %all-to-all-start = ((bf16[32,8,512]{2,1,0:T(8,128)(2,1)}), bf16[32,8,512]{2,1,0:T(8,128)(2,1)S(1)}, u32[]{:S(2)}, u32[]{:S(2)}) async-start(bf16[32,8,512]{2,1,0:T(8,128)(2,1)} %fusion.48), calls=%async_computation | async-start | bytes 524288 | tf_op jit(solution)/shard_map/all_to_all | solution.py:45
  47.1 0.1 dynamic_slice.3
  47.2 1.2 %fusion.65 = (f32[128,256]{0,1:T(8,128)S(1)}, f32[128,256]{0,1:T(8,128)}) fusion(), kind=kLoop, calls=%fused_computation.89 | loop fusion | flops 458752 | bytes 262144 | tf_op jit(solution)/shard_map/sin | solution.py:86
  48.4 1.0 fusion.61
  49.4 1.0 fusion.56
  50.4 0.1 slice_cosine_fusion
  50.6 0.6 copy-done.2
  51.2 0.8 convolution_bitcast_fusion
  51.9 17.4 %all-to-all-done = bf16[32,8,512]{2,1,0:T(8,128)(2,1)S(1)} async-done(((bf16[32,8,512]{2,1,0:T(8,128)(2,1)}), bf16[32,8,512]{2,1,0:T(8,128)(2,1)S(1)}, u32[]{:S(2)}, u32[]{:S(2)}) %all-to-all-start) | async-done | bytes 262176 | tf_op jit(solution)/shard_map/all_to_all | solution.py:45
  69.4 0.8 copy.38
  70.1 1.7 %reshape.99 = bf16[8,64,256]{2,1,0:T(8,128)(2,1)} reshape(bf16[8,32,512]{2,1,0:T(8,128)(2,1)} %copy.38) | data formatting | bytes 524288 | tf_op jit(solution)/shard_map/reshape | solution.py:104
  71.9 1.8 %convolution_bitcast_fusion.1 = f32[8,256,256]{1,2,0:T(8,128)S(1)} fusion(bf16[8,64,256]{2,1,0:T(8,128)(2,1)} %reshape.99, f32[128,64]{0,1:T(8,128)} %copy-done.4, f32[128,64]{0,1:T(8,128)} %copy-done.2), kind=kOutput, calls=%fused_computation.17 | convolution fusion | flops 201342976 | bytes 2424832 | tf_op jit(solution)/shard_map/kn,cnm->ckm/dot_general | solution.py:105
  73.7 0.6 multiply_subtract_fusion.3
  74.3 1.8 %fusion = f32[8,128,512]{2,1,0:T(8,128)S(1)} fusion(f32[8,128,256]{1,2,0:T(8,128)S(1)} %get-tuple-element.10, f32[8,128,256]{1,2,0:T(8,128)S(1)} %get-tuple-element.9, f32[256,256]{1,0:T(8,128)S(1)} %get-tuple-element.22, f32[256,256]{1,0:T(8,128)S(1)} %fusion.61, f32[256,256]{1,0:T(8,128)S(1)} %get-tuple-element.21), kind=kOutput, calls=%fused_computation | convolution fusion | flops 1611923456 | bytes 4980736 | tf_op jit(solution)/shard_map/ckn,nm->ckm/dot_general | solution.py:111
  76.1 1.8 %fusion.4 = f32[8,128,512]{2,1,0:T(8,128)S(1)} fusion(f32[8,128,256]{1,2,0:T(8,128)S(1)} %get-tuple-element.13, f32[8,128,256]{1,2,0:T(8,128)S(1)} %get-tuple-element.14, f32[256,256]{1,0:T(8,128)S(1)} %get-tuple-element.22, f32[256,256]{1,0:T(8,128)S(1)} %fusion.61, f32[256,256]{1,0:T(8,128)S(1)} %get-tuple-element.21), kind=kOutput, calls=%fused_computation.4 | convolution fusion | flops 1611923456 | bytes 4980736 | tf_op jit(solution)/shard_map/ckn,nm->ckm/dot_general | solution.py:111
  77.9 0.3 multiply_subtract_fusion.1
  78.3 1.9 %fusion.8 = f32[8,128,512]{1,2,0:T(8,128)S(1)} fusion(f32[8,128,256]{2,1,0:T(8,128)S(1)} %get-tuple-element.6, f32[8,128,256]{2,1,0:T(8,128)S(1)} %get-tuple-element.5, f32[256,256]{1,0:T(8,128)S(1)} %get-tuple-element.22, f32[256,256]{1,0:T(8,128)S(1)} %get-tuple-element.21, f32[256,256]{1,0:T(8,128)S(1)} %fusion.61), kind=kOutput, calls=%fused_computation.8 | convolution fusion | flops 1611923456 | bytes 4980736 | tf_op jit(solution)/shard_map/ckm,mn->ckn/dot_general | solution.py:119
  80.1 0.3 multiply_add_fusion
  80.5 0.4 copy-done.3
  80.9 1.1 fusion.19
  82.0 0.1 div.13
  82.1 0.3 fusion.44
  82.5 26.6 %all_to_all.26 = bf16[8,32,512]{2,0,1:T(8,128)(2,1)S(1)} all-to-all(bf16[8,32,512]{2,0,1:T(8,128)(2,1)S(1)} %fusion.44), channel_id=1, replica_groups=mesh['ctx'=32,'ch'=32] {'ctx'}, dimensions={1} | all-to-all | bytes 524288 | tf_op jit(solution)/shard_map/all_to_all | solution.py:158
  109.0 0.8 fusion.43
  (32 shorter events, 0.6 us)
Async XLA Ops:
  0.0 50.5 %copy-start = (bf16[8,16384]{1,0:T(8,128)(2,1)S(1)}, bf16[8,16384]{1,0:T(8,128)(2,1)}, u32[]{:S(2)}) copy-start(bf16[8,16384]{1,0:T(8,128)(2,1)} %param.16) | copy-start | bytes 786436
  1.2 6.1 %collective-permute-start = (bf16[256,128]{1,0:T(8,128)(2,1)S(1)}, bf16[256,128]{1,0:T(8,128)(2,1)S(1)}, u32[]{:S(2)}, u32[]{:S(2)}) collective-permute-start(bf16[256,128]{1,0:T(8,128)(2,1)S(1)} %slice.72), channel_id=1, source_target_pairs={{0,32},{32,64},{64,96},{96,128},{128,160},{160,192},{192,224},{224... | collective-permute-start | bytes 196616 | tf_op jit(solution)/shard_map/ppermute | solution.py:14
  7.3 1.0 copy-start.7
  8.3 6.0 %collective-permute-start.1 = (bf16[256,128]{1,0:T(8,128)(2,1)S(1)}, bf16[256,128]{1,0:T(8,128)(2,1)S(1)}, u32[]{:S(2)}, u32[]{:S(2)}) collective-permute-start(bf16[256,128]{1,0:T(8,128)(2,1)S(1)} %slice.74), channel_id=1, source_target_pairs={{0,32},{32,64},{64,96},{96,128},{128,160},{160,192},{192,224},{224... | collective-permute-start | bytes 196616 | tf_op jit(solution)/shard_map/ppermute | solution.py:14
  14.3 1.0 copy-start.8
  14.5 32.6 %copy-start.9 = (f32[256]{0:T(256)S(1)}, f32[256]{0:T(256)}, u32[]{:S(2)}) copy-start(f32[256]{0:T(256)} %param.17) | copy-start | bytes 3076
  16.1 53.3 %all-to-all-start = ((bf16[32,8,512]{2,1,0:T(8,128)(2,1)}), bf16[32,8,512]{2,1,0:T(8,128)(2,1)S(1)}, u32[]{:S(2)}, u32[]{:S(2)}) async-start(bf16[32,8,512]{2,1,0:T(8,128)(2,1)} %fusion.48), calls=%async_computation | async-start | bytes 524288 | tf_op jit(solution)/shard_map/all_to_all | solution.py:45
  50.5 0.6 copy-start.2
  50.5 0.6 copy-start.4
  71.9 1.8 %copy-start.1 = (f32[128,256]{0,1:T(8,128)S(1)}, f32[128,256]{0,1:T(8,128)}, u32[]{:S(2)}) copy-start(f32[128,256]{0,1:T(8,128)} %get-tuple-element.20) | copy-start | bytes 393220
  80.1 0.8 copy-start.3
  80.1 0.8 copy-start.5
  80.9 28.1 %copy-start.6 = (bf16[256,512]{1,0:T(8,128)(2,1)S(1)}, bf16[256,512]{1,0:T(8,128)(2,1)}, u32[]{:S(2)}) copy-start(bf16[256,512]{1,0:T(8,128)(2,1)} %param.13) | copy-start | bytes 786436
where the time goes:
time: 110 us
  starting transfers between devices  36.4 us (33%)
  blocking collectives  26.6 us (24%)
  waiting for transfers between devices  17.4 us (16%)
  local copies, waits for them, and re-layouts  11.2 us (10%)
  matrix products  10.1 us (9%)
  other arithmetic  7.66 us (7%)
    all_to_all x1, starting transfers between devices, to_channels(): return lax.all_to_all(data, 'ctx', split_axis=0, concat_axis=1, tiled=True)  31 us
    all_to_all x1, blocking collectives, shards(): lax.all_to_all(long_out, 'ctx', split_axis=1, concat_axis=0, tiled=True)  26.6 us
    all_to_all x1, waiting for transfers between devices, to_channels(): return lax.all_to_all(data, 'ctx', split_axis=0, concat_axis=1, tiled=True)  17.4 us
    ppermute x2, starting transfers between devices, from_behind(): return lax.ppermute(shard, axis, pairs)  5.42 us
    another operation x4, local copies, waits for them, and re-layouts, band_matrix(): tiled = jnp.tile(pattern, (1, tap_count))  3.98 us
    dot_general x2, matrix products, forward(): spectrum = jnp.einsum('ckn,nm->ckm', turned, inner_fwd, precision=HIGH)  3.66 us
    dot_general x2, matrix products, forward(): parts = jnp.einsum('kn,cnm->ckm', outer_table, grid, precision=HIGH)  2.52 us
  transfers between devices with their start and end apart: 3, of which 1 were waited for; matrix products, arithmetic and copies ran while one was open for 10% of the time, Pallas kernels for 0%

commit v1 on v0

v1 whole, which is shorter than its diff:
```python
import functools

import jax
import jax.numpy as jnp
import numpy as np
from jax import lax
from jax.experimental import pallas as pl
from jax.experimental.pallas import tpu as pltpu
from jax.sharding import PartitionSpec as P

SPLIT = False
LANES = 128
VMEM = pl.BlockSpec(memory_space=pltpu.VMEM)
SMEM = pl.BlockSpec(memory_space=pltpu.SMEM)
BF16 = jnp.bfloat16
F32 = jnp.float32


def matmul(a, b):
    return jnp.dot(a, b, preferred_element_type=F32)


def band(taps_ref, group):
    taps = taps_ref[pl.ds(group, 1), :].astype(F32)
    ring = jnp.concatenate([taps, jnp.zeros_like(taps)], axis=1)
    rows = jnp.broadcast_to(ring, (8, 2 * LANES))
    rows = pltpu.roll(rows, LANES, 1, stride=1, stride_axis=0)
    strips = [rows if m == 0 else pltpu.roll(rows, 8 * m, 1) for m in range(LANES // 8)]
    top = jnp.concatenate([s[:, :LANES] for s in strips], axis=0)
    bottom = jnp.concatenate([s[:, LANES:] for s in strips], axis=0)
    return jnp.concatenate([top, bottom], axis=0).astype(BF16)


def conv_blocks(wide, matrix, first, last):
    rows = wide.shape[0]
    stack = jnp.concatenate(
        [wide[:, b * LANES : (b + 2) * LANES] for b in range(first, last)], axis=0
    )
    out = matmul(stack, matrix)
    return jnp.concatenate([out[i * rows : (i + 1) * rows] for i in range(last - first)], axis=1)


def near_kernel(value, key, gate_one, gate_two, taps_one, taps_two, tails, kept, done, matrices):
    groups = taps_one.shape[0]
    rows = value.shape[0] // groups
    length = value.shape[1]
    for g in range(groups):
        at = pl.ds(g * rows, rows)
        matrix_one = band(taps_one, g)
        matrix_two = band(taps_two, g)
        matrices[0, g] = matrix_one
        matrices[1, g] = matrix_two
        mixed = (key[at, :].astype(F32) * value[at, :].astype(F32)).astype(BF16)
        tails[at, :LANES] = mixed[:, length - LANES :]
        first = conv_blocks(mixed, matrix_one, 0, 3)
        first = (gate_one[at, LANES:].astype(F32) * first).astype(BF16)
        tails[at, LANES:] = first[:, 2 * LANES :]
        kept[at, :] = first[:, :LANES]
        second = conv_blocks(first, matrix_two, 0, 2)
        done[at, :] = (gate_two[at, 2 * LANES :].astype(F32) * second).astype(BF16)


def edge_kernel(value, key, gate_one, gate_two, kept, matrices, halo, done, out):
    groups = matrices.shape[1]
    rows = value.shape[0] // groups
    for g in range(groups):
        at = pl.ds(g * rows, rows)
        mixed = (key[at, :].astype(F32) * value[at, :].astype(F32)).astype(BF16)
        mixed = jnp.concatenate([halo[at, :LANES], mixed], axis=1)
        first = conv_blocks(mixed, matrices[0, g], 0, 1)
        first = (gate_one[at, :].astype(F32) * first).astype(BF16)
        first = jnp.concatenate([halo[at, LANES:], first, kept[at, :]], axis=1)
        second = conv_blocks(first, matrices[1, g], 0, 2)
        second = (gate_two[at, :].astype(F32) * second).astype(BF16)
        out[at, : 2 * LANES] = second
        if not SPLIT:
            out[at, 2 * LANES :] = done[at, :]


def tables(length, devices):
    n = LANES
    per = length // n // devices
    order = np.arange(n)
    n1 = (order % devices) * per + order // devices
    k1 = np.arange(n) + 0.25
    outer = 2 * np.pi * np.outer(k1, n1) / n
    outer_table = np.concatenate([np.cos(outer), -np.sin(outer)], axis=0)
    inner = 2 * np.pi * np.outer(np.arange(n), np.arange(n)) / n
    cos, sin = np.cos(inner), np.sin(inner)
    ahead = np.block([[cos, -sin], [sin, cos]])
    back = np.block([[cos, sin], [-sin, cos]])
    turn = 2 * np.pi * np.outer(k1, np.arange(n)) / length
    half = lambda t: jnp.asarray(t, F32).astype(BF16)
    return (
        half(outer_table),
        half(outer_table.T),
        half(ahead),
        half(back),
        jnp.asarray(np.cos(turn), F32),
        jnp.asarray(np.sin(turn), F32),
    )


def transform(values, outer, ahead, cos, sin):
    n = LANES
    parts = matmul(outer[...], values)
    re, im = parts[:n], parts[n:]
    turned = jnp.concatenate([re * cos + im * sin, im * cos - re * sin], axis=1)
    return matmul(turned.astype(BF16), ahead[...])


def filter_kernel(devices, taps, outer, ahead, cos, sin, spectrum, rows):
    channels, length = taps.shape
    n = LANES
    per = length // n // devices
    scale = 1.0 / length
    for b in range(length // n):
        place = (b % per) * devices + b // per
        rows[pl.ds(place * channels, channels), :] = taps[:, b * n : (b + 1) * n].astype(F32)
    for c in range(channels):
        values = rows[pl.ds(c, n, stride=channels), :].astype(BF16)
        spectrum[c] = transform(values, outer, ahead, cos[...], sin[...]) * scale


def long_kernel(*refs):
    if SPLIT:
        late, early, spectrum, skip, outer, outer_t, ahead, back, cos, sin, out, rows, outs = refs
    else:
        early, spectrum, skip, outer, outer_t, ahead, back, cos, sin, out, rows, outs = refs
    n = LANES
    devices, channels, length = out.shape
    for part, piece in enumerate((early, late) if SPLIT else (early,)):
        width = piece.shape[2]
        flat = piece[...].astype(F32).reshape(devices * channels, width)
        for q in range(width // n):
            rows[part * (width // n) + q] = flat[:, q * n : (q + 1) * n]
    base = lax.axis_index("ctx") * channels
    cosines, sines = cos[...], sin[...]
    for c in range(channels):
        signal = jnp.concatenate(
            [
                rows[q, pl.ds(c, devices, stride=channels), :]
                for q in range(length // n)
            ],
            axis=0,
        )
        waves = transform(signal.astype(BF16), outer, ahead, cosines, sines)
        re, im = waves[:, :n], waves[:, n:]
        filter_re, filter_im = spectrum[c, :, :n], spectrum[c, :, n:]
        product = jnp.concatenate(
            [re * filter_re - im * filter_im, re * filter_im + im * filter_re], axis=1
        )
        waves = matmul(product.astype(BF16), back[...])
        re, im = waves[:, :n], waves[:, n:]
        turned = jnp.concatenate([re * cosines - im * sines, re * sines + im * cosines], axis=0)
        result = matmul(outer_t[...], turned.astype(BF16)) + skip[base + c] * signal
        for q in range(length // n):
            outs[q, pl.ds(c, devices, stride=channels), :] = result[
                q * devices : (q + 1) * devices
            ]
    for q in range(length // n):
        block = outs[q].reshape(devices, channels, n)
        out[:, :, q * n : (q + 1) * n] = block.astype(BF16)


def shards(
    value_in,
    key_in,
    gate_first,
    gate_second,
    gate_long,
    filter_first,
    filter_second,
    long_filter,
    skip_gain,
):
    channels, length = value_in.shape
    devices = lax.axis_size("ctx")
    per = channels // devices
    groups = filter_first.shape[0]
    total = length * devices
    half = length // 2
    shape = jax.ShapeDtypeStruct

    tails, kept, late, matrices = pl.pallas_call(
        near_kernel,
        out_shape=(
            shape((channels, 2 * LANES), BF16),
            shape((channels, LANES), BF16),
            shape((channels, half), BF16),
            shape((2, groups, 2 * LANES, LANES), BF16),
        ),
        in_specs=[VMEM] * 6,
        out_specs=(VMEM,) * 4,
        name="near",
    )(value_in, key_in, gate_first, gate_second, filter_first, filter_second)
    halo = lax.ppermute(tails, "ctx", [(i, i + 1) for i in range(devices - 1)])

    outer, outer_t, ahead, back, cos, sin = tables(total, devices)
    spectrum = pl.pallas_call(
        functools.partial(filter_kernel, devices),
        out_shape=shape((per, LANES, 2 * LANES), F32),
        in_specs=[VMEM] * 5,
        out_specs=VMEM,
        scratch_shapes=[pltpu.VMEM((LANES * per, LANES), F32)],
        name="spectrum",
    )(long_filter, outer, ahead, cos, sin)

    width = half if SPLIT else length
    early = pl.pallas_call(
        edge_kernel,
        out_shape=shape((channels, width), BF16),
        grid=(1,),
        in_specs=[
            pl.BlockSpec((channels, half), lambda i: (0, 0)),
            pl.BlockSpec((channels, half), lambda i: (0, 0)),
            pl.BlockSpec((channels, LANES), lambda i: (0, 0)),
            pl.BlockSpec((channels, half), lambda i: (0, 0)),
            VMEM,
            VMEM,
            VMEM,
            VMEM,
        ],
        out_specs=VMEM,
        name="edge",
    )(value_in, key_in, gate_first, gate_second, kept, matrices, halo, late)

    def swap(data):
        return lax.all_to_all(data, "ctx", split_axis=0, concat_axis=0, tiled=True)

    moved = [swap(early.reshape(devices, per, width))]
    if SPLIT:
        moved = [swap(late.reshape(devices, per, half))] + moved
    long_out = pl.pallas_call(
        long_kernel,
        out_shape=shape((devices, per, length), BF16),
        in_specs=[VMEM] * len(moved) + [VMEM, SMEM] + [VMEM] * 6,
        out_specs=VMEM,
        scratch_shapes=[
            pltpu.VMEM((length // LANES, devices * per, LANES), F32),
            pltpu.VMEM((length // LANES, devices * per, LANES), F32),
        ],
        name="long",
    )(*moved, spectrum, skip_gain, outer, outer_t, ahead, back, cos, sin)
    back_home = swap(long_out).reshape(channels, length)
    return (gate_long.astype(F32) * back_home.astype(F32)).astype(BF16)


def solution(mesh):
    placed = (
        P("ch", "ctx"),
        P("ch", "ctx"),
        P("ch", "ctx"),
        P("ch", "ctx"),
        P("ch", "ctx"),
        P("ch", None),
        P("ch", None),
        P(("ch", "ctx"), None),
        P("ch"),
    )
    return jax.shard_map(
        shards, mesh=mesh, in_specs=placed, out_specs=P("ch", "ctx"), check_vma=False
    )
```

time: 110 us -> 97.3 us (0.88)
  the two profiles are of different devices: /device:TPU:10 before, /device:TPU:65 now
where the time goes in v1:
time: 97.3 us; the launch traced here: 97 us
  starting transfers between devices  32.4 us (33%)
  blocking collectives  26.2 us (27%)
  waiting for transfers between devices  21.6 us (22%)
  Pallas kernels  14.7 us (15%)
  local copies, waits for them, and re-layouts  1.35 us (1%)
    all_to_all x1, starting transfers between devices, swap(): return lax.all_to_all(data, 'ctx', split_axis=0, concat_axis=0, tiled=True)  28.7 us
    all_to_all x1, blocking collectives, swap(): return lax.all_to_all(data, 'ctx', split_axis=0, concat_axis=0, tiled=True)  26.2 us
    all_to_all x1, waiting for transfers between devices, swap(): return lax.all_to_all(data, 'ctx', split_axis=0, concat_axis=0, tiled=True)  19.4 us
    pallas_call x1, Pallas kernels, shards(): pl.pallas_call(long_kernel, out_shape=shape((devices, per, length), BF16)...  4.9 us
    pallas_call x1, Pallas kernels, shards(): pl.pallas_call(near_kernel, out_shape=(shape((channels, 2 * LANES), BF16)...  4.11 us
    ppermute x1, starting transfers between devices, shards(): halo = lax.ppermute(tails, 'ctx', [(i, i + 1) for i in range(devices - 1)])  3.67 us
    pallas_call x1, Pallas kernels, shards(): pl.pallas_call(edge_kernel, out_shape=shape((channels, width), BF16), gri...  3.01 us
    pallas_call x1, Pallas kernels, shards(): pl.pallas_call(functools.partial(filter_kernel, devices), out_shape=shape...  2.64 us
  transfers between devices with their start and end apart: 2, of which 2 were waited for; matrix products, arithmetic and copies ran while one was open for 0% of the time, Pallas kernels for 3%

profile of v1, /device:TPU:65, one launch (start us, length us, event | category | flops | bytes accessed | tf_op | source)
XLA Modules:
  0.0 97.0 jit_solution(8596192766224545492)
XLA Ops:
  0.0 4.1 %near.1 = (bf16[256,256]{1,0:T(8,128)(2,1)}, bf16[256,128]{1,0:T(8,128)(2,1)}, bf16[256,256]{1,0:T(8,128)(2,1)}, bf16[2,16,256,128]{3,2,1,0:T(8,128)(2,1)}) custom-call(bf16[256,512]{1,0:T(8,128)(2,1)} %value.3, bf16[256,512]{1,0:T(8,128)(2,1)} %key.3, bf16[256,512]{1,0:T(8,128)(2,1)} %gate_one.3, bf16[256,512]{1,0:T(8,128)(2,1)} %gate_two.3, ...), custom_call_target="tpu_custom_call" | custom-call | tf_op jit(solution)/shard_map/near/pallas_call | solution.py:185
  4.1 3.7 %collective-permute-start = (bf16[256,256]{1,0:T(8,128)(2,1)}, bf16[256,256]{1,0:T(8,128)(2,1)S(1)}, u32[]{:S(2)}, u32[]{:S(2)}) collective-permute-start(bf16[256,256]{1,0:T(8,128)(2,1)} %get-tuple-element.11), channel_id=1, source_target_pairs={{0,32},{32,64},{64,96},{96,128},{128,160},{160,192},{192,224},{224... | collective-permute-start | bytes 393224 | tf_op jit(solution)/shard_map/ppermute | solution.py:197
  7.8 2.2 %collective-permute-done.halo = bf16[256,256]{1,0:T(8,128)(2,1)S(1)} collective-permute-done((bf16[256,256]{1,0:T(8,128)(2,1)}, bf16[256,256]{1,0:T(8,128)(2,1)S(1)}, u32[]{:S(2)}, u32[]{:S(2)}) %collective-permute-start) | collective-permute-done | bytes 131104 | tf_op jit(solution)/shard_map/ppermute | solution.py:197
  10.0 0.0 copy-start.2
  10.0 0.6 copy-done.2
  10.7 3.0 %edge.1 = bf16[256,512]{1,0:T(8,128)(2,1)} custom-call(bf16[256,512]{1,0:T(8,128)(2,1)} %value.3, bf16[256,512]{1,0:T(8,128)(2,1)} %key.3, bf16[256,512]{1,0:T(8,128)(2,1)} %gate_one.3, bf16[256,512]{1,0:T(8,128)(2,1)} %gate_two.3, bf16[256,128]{1,0:T(8,128)(2,1)} %get-tuple-element.9.kept, bf16[2,16,256,128]{3,2,1,0:T(8,128)(2,1)} %get-tuple-element.10.matrices, ...), custom_call_target="tpu_custom_call" | custom-call | tf_op jit(solution)/shard_map/edge/pallas_call | solution.py:210
  13.7 28.7 %all-to-all-start = ((bf16[32,8,512]{2,1,0:T(8,128)(2,1)}), bf16[32,8,512]{2,1,0:T(8,128)(2,1)S(1)}, u32[]{:S(2)}, u32[]{:S(2)}) async-start(bf16[32,8,512]{2,1,0:T(8,128)(2,1)} %bitcast.4), calls=%async_computation | async-start | bytes 524288 | tf_op jit(solution)/shard_map/all_to_all | solution.py:229
  42.4 0.0 copy-start.1
  42.4 2.6 %spectrum.1.refs_1_ = f32[8,128,256]{2,1,0:T(8,128)} custom-call(bf16[8,16384]{1,0:T(8,128)(2,1)} %taps.1, bf16[256,128]{1,0:T(8,128)(2,1)} %constant.21.outer.refs_3_, bf16[256,256]{1,0:T(8,128)(2,1)} %constant.22.ahead.refs_5_, f32[128,128]{1,0:T(8,128)} %constant.16.clone.cos.refs_7_, f32[128,128]{1,0:T(8,128)} %constant.17.clone.sin.refs_8_), custom_call_target="tpu_custom_call" | custom-call | tf_op jit(solution)/shard_map/spectrum/pallas_call | solution.py:200
  45.0 19.4 %all-to-all-done.refs_0_ = bf16[32,8,512]{2,1,0:T(8,128)(2,1)S(1)} async-done(((bf16[32,8,512]{2,1,0:T(8,128)(2,1)}), bf16[32,8,512]{2,1,0:T(8,128)(2,1)S(1)}, u32[]{:S(2)}, u32[]{:S(2)}) %all-to-all-start) | async-done | bytes 262176 | tf_op jit(solution)/shard_map/all_to_all | solution.py:229
  64.4 0.0 copy-start
  64.4 0.7 copy-done
  65.1 4.9 %long.1 = bf16[32,8,512]{2,1,0:T(8,128)(2,1)} custom-call(bf16[32,8,512]{2,1,0:T(8,128)(2,1)} %copy-done, f32[8,128,256]{2,1,0:T(8,128)} %spectrum.1.refs_1_, f32[256]{0:T(256)} %refs_2_.1, bf16[256,128]{1,0:T(8,128)(2,1)} %constant.21.outer.refs_3_, bf16[128,256]{1,0:T(8,128)(2,1)} %constant.23.refs_4_, bf16[256,256]{1,0:T(8,128)(2,1)} %constant.22.ahead.refs_5_, ...), custom_call_target="tpu_custom_call" | custom-call | tf_op jit(solution)/shard_map/long/pallas_call | solution.py:234
  70.0 26.2 %all_to_all.10 = bf16[32,8,512]{2,1,0:T(8,128)(2,1)S(1)} all-to-all(bf16[32,8,512]{2,1,0:T(8,128)(2,1)} %long.1), channel_id=1, replica_groups=mesh['ctx'=32,'ch'=32] {'ctx'}, dimensions={0} | all-to-all | bytes 524288 | tf_op jit(solution)/shard_map/all_to_all | solution.py:229
  96.2 0.0 copy-done.1
  96.2 0.8 fusion
Async XLA Ops:
  4.1 5.9 %collective-permute-start = (bf16[256,256]{1,0:T(8,128)(2,1)}, bf16[256,256]{1,0:T(8,128)(2,1)S(1)}, u32[]{:S(2)}, u32[]{:S(2)}) collective-permute-start(bf16[256,256]{1,0:T(8,128)(2,1)} %get-tuple-element.11), channel_id=1, source_target_pairs={{0,32},{32,64},{64,96},{96,128},{128,160},{160,192},{192,224},{224... | collective-permute-start | bytes 393224 | tf_op jit(solution)/shard_map/ppermute | solution.py:197
  10.0 0.6 copy-start.2
  13.7 50.8 %all-to-all-start = ((bf16[32,8,512]{2,1,0:T(8,128)(2,1)}), bf16[32,8,512]{2,1,0:T(8,128)(2,1)S(1)}, u32[]{:S(2)}, u32[]{:S(2)}) async-start(bf16[32,8,512]{2,1,0:T(8,128)(2,1)} %bitcast.4), calls=%async_computation | async-start | bytes 524288 | tf_op jit(solution)/shard_map/all_to_all | solution.py:229
  42.4 53.8 %copy-start.1 = (bf16[256,512]{1,0:T(8,128)(2,1)S(1)}, bf16[256,512]{1,0:T(8,128)(2,1)}, u32[]{:S(2)}) copy-start(bf16[256,512]{1,0:T(8,128)(2,1)} %param.19) | copy-start | bytes 786436
  64.4 0.7 copy-start

commit v2 on v1

v2 whole, which is shorter than its diff:
```python
import jax
import jax.numpy as jnp
import numpy as np
from jax import lax
from jax.experimental import pallas as pl
from jax.experimental.pallas import tpu as pltpu
from jax.sharding import PartitionSpec as P

SPLIT = False
LANES = 128
VMEM = pl.BlockSpec(memory_space=pltpu.VMEM)
SMEM = pl.BlockSpec(memory_space=pltpu.SMEM)
BF16 = jnp.bfloat16
F32 = jnp.float32


def near_core(data):
    return pltpu.with_memory_space_constraint(data, pltpu.VMEM)


def in_hbm(data):
    return pltpu.with_memory_space_constraint(data, pltpu.HBM)


def call(kernel, outs, name, *args, specs=None, scratch=()):
    return pl.pallas_call(
        kernel,
        out_shape=outs,
        grid=(1,),
        in_specs=specs or [VMEM] * len(args),
        out_specs=(VMEM,) * len(outs) if isinstance(outs, tuple) else VMEM,
        scratch_shapes=list(scratch),
        compiler_params=pltpu.CompilerParams(vmem_limit_bytes=16 << 20),
        name=name,
    )(*args)


def matmul(a, b):
    return jnp.dot(a, b, preferred_element_type=F32)


def band(taps_ref, group):
    taps = taps_ref[pl.ds(group, 1), :].astype(F32)
    ring = jnp.concatenate([taps, jnp.zeros_like(taps)], axis=1)
    rows = jnp.broadcast_to(ring, (8, 2 * LANES))
    rows = pltpu.roll(rows, LANES, 1, stride=1, stride_axis=0)
    strips = [rows if m == 0 else pltpu.roll(rows, 8 * m, 1) for m in range(LANES // 8)]
    top = jnp.concatenate([s[:, :LANES] for s in strips], axis=0)
    bottom = jnp.concatenate([s[:, LANES:] for s in strips], axis=0)
    return jnp.concatenate([top, bottom], axis=0).astype(BF16)


def conv_blocks(wide, matrix, first, last):
    rows = wide.shape[0]
    stack = jnp.concatenate(
        [wide[:, b * LANES : (b + 2) * LANES] for b in range(first, last)], axis=0
    )
    out = matmul(stack, matrix)
    return jnp.concatenate([out[i * rows : (i + 1) * rows] for i in range(last - first)], axis=1)


def tail_kernel(value, key, gate_one, gate_two, taps, tails, matrices, mixed, one, two):
    groups = taps.shape[0]
    rows = value.shape[0] // groups
    width = mixed.shape[1]
    for g in range(groups):
        at = pl.ds(g * rows, rows)
        matrix = band(taps, g)
        matrices[g] = matrix
        block = (key[at, :].astype(F32) * value[at, :].astype(F32)).astype(BF16)
        tails[at, :LANES] = block[:, width:]
        first = conv_blocks(block[:, width - LANES :], matrix, 0, 1)
        tails[at, LANES:] = (gate_one[at, width:].astype(F32) * first).astype(BF16)
        mixed[at, :] = block[:, :width]
    one[...] = gate_one[:, :width]
    two[...] = gate_two[...]


def near_kernel(mixed, gate_one, gate_two, ahead, taps, tails, kept, out, matrices):
    groups = taps.shape[0]
    rows = mixed.shape[0] // groups
    for g in range(groups):
        at = pl.ds(g * rows, rows)
        matrix = band(taps, g)
        matrices[g] = matrix
        first = conv_blocks(mixed[at, :], ahead[g], 0, 2)
        first = (gate_one[at, LANES:].astype(F32) * first).astype(BF16)
        kept[at, :] = first[:, :LANES]
        first = jnp.concatenate([first, tails[at, LANES:]], axis=1)
        second = conv_blocks(first, matrix, 0, 2)
        out[at, :] = (gate_two[at, 2 * LANES :].astype(F32) * second).astype(BF16)


def edge_kernel(mixed, gate_one, gate_two, kept, matrices_one, matrices_two, halo, *refs):
    out = refs[-1]
    groups = matrices_one.shape[0]
    rows = mixed.shape[0] // groups
    for g in range(groups):
        at = pl.ds(g * rows, rows)
        first = jnp.concatenate([halo[at, :LANES], mixed[at, :LANES]], axis=1)
        first = conv_blocks(first, matrices_one[g], 0, 1)
        first = (gate_one[at, :LANES].astype(F32) * first).astype(BF16)
        first = jnp.concatenate([halo[at, LANES:], first, kept[at, :]], axis=1)
        second = conv_blocks(first, matrices_two[g], 0, 2)
        out[at, : 2 * LANES] = (gate_two[at, : 2 * LANES].astype(F32) * second).astype(BF16)
        if not SPLIT:
            out[at, 2 * LANES :] = refs[0][at, :]


def tables(length, devices):
    n = LANES
    per = length // n // devices
    order = np.arange(n)
    n1 = (order % devices) * per + order // devices
    k1 = np.arange(n) + 0.25
    outer = 2 * np.pi * np.outer(k1, n1) / n
    outer_table = np.concatenate([np.cos(outer), -np.sin(outer)], axis=0)
    inner = 2 * np.pi * np.outer(np.arange(n), np.arange(n)) / n
    cos, sin = np.cos(inner), np.sin(inner)
    ahead = np.block([[cos, -sin], [sin, cos]])
    back = np.block([[cos, sin], [-sin, cos]])
    turn = 2 * np.pi * np.outer(k1, np.arange(n)) / length
    half = lambda t: jnp.asarray(t, F32).astype(BF16)
    return (
        half(outer_table),
        half(outer_table.T),
        half(ahead),
        half(back),
        jnp.asarray(np.cos(turn), F32),
        jnp.asarray(np.sin(turn), F32),
    )


def gather_rows(rows, channel, channels):
    count = rows.shape[1] // channels
    picked = [rows[q, pl.ds(channel, count, stride=channels), :] for q in range(rows.shape[0])]
    return jnp.concatenate(picked, axis=0)


def transform(signals, outer, ahead, cos, sin):
    n = LANES
    parts = matmul(outer, jnp.concatenate([s.astype(BF16) for s in signals], axis=1))
    turned = []
    for c in range(len(signals)):
        re, im = parts[:n, c * n : (c + 1) * n], parts[n:, c * n : (c + 1) * n]
        both = jnp.concatenate([re * cos + im * sin, im * cos - re * sin], axis=1)
        turned.append(both.astype(BF16))
    return matmul(jnp.concatenate(turned, axis=0), ahead)


def filter_kernel(taps, outer, ahead, cos, sin, spectrum, rows):
    channels, length = taps.shape
    n = LANES
    per = rows.shape[0]
    for b in range(length // n):
        at = pl.ds(b // per * channels, channels)
        rows[b % per, at, :] = taps[:, b * n : (b + 1) * n].astype(F32)
    signals = [gather_rows(rows, c, channels) for c in range(channels)]
    waves = transform(signals, outer[...], ahead[...], cos[...], sin[...])
    spectrum[...] = (waves * (1.0 / length)).reshape(spectrum.shape)


def long_kernel(*refs):
    if SPLIT:
        late, early, spectrum, skip, outer, outer_t, ahead, back, cos, sin, out, rows, outs = refs
    else:
        early, spectrum, skip, outer, outer_t, ahead, back, cos, sin, out, rows, outs = refs
    n = LANES
    devices, channels, length = out.shape
    for part, piece in enumerate((early, late) if SPLIT else (early,)):
        width = piece.shape[2]
        flat = piece[...].astype(F32).reshape(devices * channels, width)
        for q in range(width // n):
            rows[part * (width // n) + q] = flat[:, q * n : (q + 1) * n]
    base = lax.axis_index("ctx") * channels
    cosines, sines = cos[...], sin[...]
    signals = [gather_rows(rows, c, channels) for c in range(channels)]
    waves = transform(signals, outer[...], ahead[...], cosines, sines)
    products = []
    for c in range(channels):
        re, im = waves[c * n : (c + 1) * n, :n], waves[c * n : (c + 1) * n, n:]
        filter_re, filter_im = spectrum[c, :, :n], spectrum[c, :, n:]
        both = [re * filter_re - im * filter_im, re * filter_im + im * filter_re]
        products.append(jnp.concatenate(both, axis=1).astype(BF16))
    waves = matmul(jnp.concatenate(products, axis=0), back[...])
    turned = []
    for c in range(channels):
        re, im = waves[c * n : (c + 1) * n, :n], waves[c * n : (c + 1) * n, n:]
        both = [re * cosines - im * sines, re * sines + im * cosines]
        turned.append(jnp.concatenate(both, axis=0).astype(BF16))
    results = matmul(outer_t[...], jnp.concatenate(turned, axis=1))
    for c in range(channels):
        result = results[:, c * n : (c + 1) * n] + skip[base + c] * signals[c]
        for q in range(length // n):
            at = pl.ds(c, devices, stride=channels)
            outs[q, at, :] = result[q * devices : (q + 1) * devices]
    for q in range(length // n):
        block = outs[q].reshape(devices, channels, n)
        out[:, :, q * n : (q + 1) * n] = block.astype(BF16)


def shards(
    value_in,
    key_in,
    gate_first,
    gate_second,
    gate_long,
    filter_first,
    filter_second,
    long_filter,
    skip_gain,
):
    channels, length = value_in.shape
    devices = lax.axis_size("ctx")
    per = channels // devices
    groups = filter_first.shape[0]
    half = length // 2
    outer, outer_t, ahead, back, cos, sin = [near_core(t) for t in tables(length * devices, devices)]
    bands = pltpu.VMEM((groups, 2 * LANES, LANES), BF16)
    width = length - LANES
    tails, ones, mixed, gate_one, gate_two = call(
        tail_kernel,
        (
            pltpu.VMEM((channels, 2 * LANES), BF16),
            bands,
            pltpu.VMEM((channels, width), BF16),
            pltpu.VMEM((channels, width), BF16),
            pltpu.VMEM((channels, length), BF16),
        ),
        "tail",
        *map(in_hbm, (value_in, key_in, gate_first, gate_second, filter_first)),
    )
    halo = lax.ppermute(tails, "ctx", [(i, i + 1) for i in range(devices - 1)])
    mixed, gate_one, gate_two, ones = map(near_core, (mixed, gate_one, gate_two, ones))
    kept, late, twos = call(
        near_kernel,
        (
            pltpu.VMEM((channels, LANES), BF16),
            pltpu.VMEM((channels, half), BF16),
            bands,
        ),
        "near",
        mixed,
        gate_one,
        gate_two,
        ones,
        near_core(filter_second),
        near_core(tails),
    )
    width = half if SPLIT else length
    rest = () if SPLIT else (near_core(late),)
    early = call(
        edge_kernel,
        pltpu.VMEM((channels, width), BF16),
        "edge",
        mixed,
        gate_one,
        gate_two,
        near_core(kept),
        ones,
        near_core(twos),
        near_core(halo),
        *rest,
    )
    plane = pltpu.VMEM((length // LANES, devices * per, LANES), F32)
    spectrum = call(
        filter_kernel,
        pltpu.VMEM((per, LANES, 2 * LANES), F32),
        "spectrum",
        near_core(long_filter),
        outer,
        ahead,
        cos,
        sin,
        scratch=[plane],
    )

    def swap(data):
        return lax.all_to_all(data, "ctx", split_axis=0, concat_axis=0, tiled=True)

    moved = [swap(early.reshape(devices, per, width))]
    if SPLIT:
        moved = [swap(late.reshape(devices, per, half))] + moved
    long_out = call(
        long_kernel,
        pltpu.VMEM((devices, per, length), BF16),
        "long",
        *map(near_core, moved),
        near_core(spectrum),
        skip_gain,
        outer,
        outer_t,
        ahead,
        back,
        cos,
        sin,
        specs=[VMEM] * (len(moved) + 1) + [SMEM] + [VMEM] * 6,
        scratch=[plane, plane],
    )
    back_home = swap(long_out).reshape(channels, length)
    return (gate_long.astype(F32) * back_home.astype(F32)).astype(BF16)


def solution(mesh):
    placed = (
        P("ch", "ctx"),
        P("ch", "ctx"),
        P("ch", "ctx"),
        P("ch", "ctx"),
        P("ch", "ctx"),
        P("ch", None),
        P("ch", None),
        P(("ch", "ctx"), None),
        P("ch"),
    )
    return jax.shard_map(
        shards, mesh=mesh, in_specs=placed, out_specs=P("ch", "ctx"), check_vma=False
    )
```

time: 97.3 us -> 88.8 us (0.913)
  Pallas kernels: 14.7 us -> 6.06 us
  local copies, waits for them, and re-layouts: 1.35 us -> 0.05 us
  waiting for transfers between devices: 21.6 us -> 22.6 us
    pallas_call x4 -> x5, Pallas kernels: 14.7 us -> 6.06 us  [call(): pl.pallas_call(kernel, out_shape=outs, grid=(1,), in_specs=specs or [VMEM...]
    all_to_all x1, waiting for transfers between devices: 19.4 us -> 21.4 us  [swap(): return lax.all_to_all(data, 'ctx', split_axis=0, concat_axis=0, tiled=True)]
    unnamed x6 -> x20, local copies, waits for them, and re-layouts: 1.35 us -> 0.05 us
    ppermute x1, waiting for transfers between devices: 2.24 us -> 1.2 us  [shards(): halo = lax.ppermute(tails, 'ctx', [(i, i + 1) for i in range(devices - 1)])]
  transfers between devices with their start and end apart: 2 -> 2, of which waited for: 2 -> 2; matrix products, arithmetic and copies ran while one was open for 0% -> 0% of each run, Pallas kernels for 3% -> 1%
where the time goes in v2:
time: 88.8 us; the launch traced here: 88.5 us
  starting transfers between devices  32.8 us (37%)
  blocking collectives  26.1 us (29%)
  waiting for transfers between devices  22.6 us (25%)
  Pallas kernels  6.06 us (7%)
    all_to_all x1, starting transfers between devices, swap(): return lax.all_to_all(data, 'ctx', split_axis=0, concat_axis=0, tiled=True)  29 us
    all_to_all x1, blocking collectives, swap(): return lax.all_to_all(data, 'ctx', split_axis=0, concat_axis=0, tiled=True)  26.1 us
    all_to_all x1, waiting for transfers between devices, swap(): return lax.all_to_all(data, 'ctx', split_axis=0, concat_axis=0, tiled=True)  21.4 us
    pallas_call x5, Pallas kernels, call(): pl.pallas_call(kernel, out_shape=outs, grid=(1,), in_specs=specs or [VMEM...  6.06 us
    ppermute x1, starting transfers between devices, shards(): halo = lax.ppermute(tails, 'ctx', [(i, i + 1) for i in range(devices - 1)])  3.81 us
  transfers between devices with their start and end apart: 2, of which 2 were waited for; matrix products, arithmetic and copies ran while one was open for 0% of the time, Pallas kernels for 1%

profile of v2, /device:TPU:65, one launch (start us, length us, event | category | flops | bytes accessed | tf_op | source)
XLA Modules:
  0.0 88.5 jit_solution(9457772620539533746)
XLA Ops:
  0.0 2.1 %tail.1 = (bf16[256,256]{1,0:T(8,128)(2,1)S(1)}, bf16[16,256,128]{2,1,0:T(8,128)(2,1)S(1)}, bf16[256,384]{1,0:T(8,128)(2,1)S(1)}, bf16[256,384]{1,0:T(8,128)(2,1)S(1)}, bf16[256,512]{1,0:T(8,128)(2,1)S(1)}) custom-call(bf16[256,512]{1,0:T(8,128)(2,1)} %value.1, bf16[256,512]{1,0:T(8,128)(2,1)} %key.1, bf16[256,512]{1,0:T(8,128)(2,1)} %gate_one.1, ...), custom_call_target="tpu_custom_call" | custom-call | tf_op jit(solution)/shard_map/tail/pallas_call | solution.py:26
  2.1 0.0 copy-start.7
  2.1 3.8 %collective-permute-start = (bf16[256,256]{1,0:T(8,128)(2,1)S(1)}, bf16[256,256]{1,0:T(8,128)(2,1)S(1)}, u32[]{:S(2)}, u32[]{:S(2)}) collective-permute-start(bf16[256,256]{1,0:T(8,128)(2,1)S(1)} %get-tuple-element.17.tails), channel_id=1, source_target_pairs={{0,32},{32,64},{64,96},{96,128},{128,160},{160,192},{192,224},{224... | collective-permute-start | bytes 393224 | tf_op jit(solution)/shard_map/ppermute | solution.py:233
  5.9 0.0 copy-done.7
  5.9 0.7 near.1
  6.6 1.2 %collective-permute-done.halo = bf16[256,256]{1,0:T(8,128)(2,1)S(1)} collective-permute-done((bf16[256,256]{1,0:T(8,128)(2,1)S(1)}, bf16[256,256]{1,0:T(8,128)(2,1)S(1)}, u32[]{:S(2)}, u32[]{:S(2)}) %collective-permute-start) | collective-permute-done | bytes 131104 | tf_op jit(solution)/shard_map/ppermute | solution.py:233
  7.8 0.0 copy-start.4
  7.8 1.2 %edge.1 = bf16[256,512]{1,0:T(8,128)(2,1)} custom-call(bf16[256,384]{1,0:T(8,128)(2,1)S(1)} %get-tuple-element.13.mixed, bf16[256,384]{1,0:T(8,128)(2,1)S(1)} %get-tuple-element.14.gate_one, bf16[256,512]{1,0:T(8,128)(2,1)S(1)} %get-tuple-element.15.gate_two, bf16[256,128]{1,0:T(8,128)(2,1)S(1)} %get-tuple-element.18.kept, ...), custom_call_target="tpu_custom_call" | custom-call | tf_op jit(solution)/shard_map/edge/pallas_call | solution.py:26
  9.1 0.0 copy-start
  9.1 0.0 copy-start.1
  9.1 0.0 copy-start.2
  9.1 0.0 copy-start.3
  9.1 29.0 %all-to-all-start = ((bf16[32,8,512]{2,1,0:T(8,128)(2,1)}), bf16[32,8,512]{2,1,0:T(8,128)(2,1)S(1)}, u32[]{:S(2)}, u32[]{:S(2)}) async-start(bf16[32,8,512]{2,1,0:T(8,128)(2,1)} %bitcast), calls=%async_computation | async-start | bytes 524288 | tf_op jit(solution)/shard_map/all_to_all | solution.py:279
  38.0 0.0 copy-done.4
  38.0 0.0 copy-done
  38.0 0.0 copy-done.1
  38.1 0.0 copy-done.2
  38.1 0.0 copy-done.3
  38.1 0.0 copy-start.5
  38.1 0.0 copy-start.6
  38.1 0.0 copy-start.8
  38.1 0.5 spectrum.1.refs_1_
  38.7 21.4 %all-to-all-done.refs_0_ = bf16[32,8,512]{2,1,0:T(8,128)(2,1)S(1)} async-done(((bf16[32,8,512]{2,1,0:T(8,128)(2,1)}), bf16[32,8,512]{2,1,0:T(8,128)(2,1)S(1)}, u32[]{:S(2)}, u32[]{:S(2)}) %all-to-all-start) | async-done | bytes 262176 | tf_op jit(solution)/shard_map/all_to_all | solution.py:279
  60.1 0.0 copy-done.5
  60.1 0.0 copy-done.6
  60.1 0.0 copy-done.8
  60.1 1.5 %long.1 = bf16[32,8,512]{2,1,0:T(8,128)(2,1)S(1)} custom-call(bf16[32,8,512]{2,1,0:T(8,128)(2,1)S(1)} %all-to-all-done.refs_0_, f32[8,128,256]{2,1,0:T(8,128)S(1)} %spectrum.1.refs_1_, f32[256]{0:T(256)S(1)} %copy-done.8, bf16[256,128]{1,0:T(8,128)(2,1)S(1)} %copy-done.4, bf16[128,256]{1,0:T(8,128)(2,1)S(1)} %copy-done.6, bf16[256,256]{1,0:T(8,128)(2,1)S(1)} %copy-done, ...), custom_call_target="tpu_custom_call" | custom-call | tf_op jit(solution)/shard_map/long/pallas_call | solution.py:26
  61.6 0.0 copy-start.9
  61.6 26.1 %all_to_all.10 = bf16[32,8,512]{2,1,0:T(8,128)(2,1)S(1)} all-to-all(bf16[32,8,512]{2,1,0:T(8,128)(2,1)S(1)} %long.1), channel_id=1, replica_groups=mesh['ctx'=32,'ch'=32] {'ctx'}, dimensions={0} | all-to-all | bytes 524288 | tf_op jit(solution)/shard_map/all_to_all | solution.py:279
  87.7 0.0 copy-done.9
  87.7 0.8 fusion
Async XLA Ops:
  2.1 3.8 %copy-start.7 = (bf16[16,128]{1,0:T(8,128)(2,1)S(1)}, bf16[16,128]{1,0:T(8,128)(2,1)}, u32[]{:S(2)}) copy-start(bf16[16,128]{1,0:T(8,128)(2,1)} %taps.4) | copy-start | bytes 12292
  2.1 5.7 %collective-permute-start = (bf16[256,256]{1,0:T(8,128)(2,1)S(1)}, bf16[256,256]{1,0:T(8,128)(2,1)S(1)}, u32[]{:S(2)}, u32[]{:S(2)}) collective-permute-start(bf16[256,256]{1,0:T(8,128)(2,1)S(1)} %get-tuple-element.17.tails), channel_id=1, source_target_pairs={{0,32},{32,64},{64,96},{96,128},{128,160},{160,192},{192,224},{224... | collective-permute-start | bytes 393224 | tf_op jit(solution)/shard_map/ppermute | solution.py:233
  7.8 30.2 %copy-start.4 = (bf16[256,128]{1,0:T(8,128)(2,1)S(1)}, bf16[256,128]{1,0:T(8,128)(2,1)}, u32[]{:S(2)}) copy-start(bf16[256,128]{1,0:T(8,128)(2,1)} %constant.21.outer.refs_3_) | copy-start | bytes 196612
  9.1 29.0 %copy-start = (bf16[256,256]{1,0:T(8,128)(2,1)S(1)}, bf16[256,256]{1,0:T(8,128)(2,1)}, u32[]{:S(2)}) copy-start(bf16[256,256]{1,0:T(8,128)(2,1)} %constant.22.ahead.refs_5_) | copy-start | bytes 393220
  9.1 29.0 %copy-start.1 = (bf16[8,16384]{1,0:T(8,128)(2,1)S(1)}, bf16[8,16384]{1,0:T(8,128)(2,1)}, u32[]{:S(2)}) copy-start(bf16[8,16384]{1,0:T(8,128)(2,1)} %taps.5) | copy-start | bytes 786436
  9.1 29.0 %copy-start.2 = (f32[128,128]{1,0:T(8,128)S(1)}, f32[128,128]{1,0:T(8,128)}, u32[]{:S(2)}) copy-start(f32[128,128]{1,0:T(8,128)} %constant.16.clone.cos.refs_7_) | copy-start | bytes 196612
  9.1 29.0 %copy-start.3 = (f32[128,128]{1,0:T(8,128)S(1)}, f32[128,128]{1,0:T(8,128)}, u32[]{:S(2)}) copy-start(f32[128,128]{1,0:T(8,128)} %constant.17.clone.sin.refs_8_) | copy-start | bytes 196612
  9.1 51.0 %all-to-all-start = ((bf16[32,8,512]{2,1,0:T(8,128)(2,1)}), bf16[32,8,512]{2,1,0:T(8,128)(2,1)S(1)}, u32[]{:S(2)}, u32[]{:S(2)}) async-start(bf16[32,8,512]{2,1,0:T(8,128)(2,1)} %bitcast), calls=%async_computation | async-start | bytes 524288 | tf_op jit(solution)/shard_map/all_to_all | solution.py:279
  38.1 22.0 %copy-start.5 = (bf16[256,256]{1,0:T(8,128)(2,1)S(1)}, bf16[256,256]{1,0:T(8,128)(2,1)}, u32[]{:S(2)}) copy-start(bf16[256,256]{1,0:T(8,128)(2,1)} %constant.24.refs_6_) | copy-start | bytes 393220
  38.1 22.0 %copy-start.6 = (bf16[128,256]{1,0:T(8,128)(2,1)S(1)}, bf16[128,256]{1,0:T(8,128)(2,1)}, u32[]{:S(2)}) copy-start(bf16[128,256]{1,0:T(8,128)(2,1)} %constant.23.refs_4_) | copy-start | bytes 196612
  38.1 22.0 %copy-start.8 = (f32[256]{0:T(256)S(1)}, f32[256]{0:T(256)}, u32[]{:S(2)}) copy-start(f32[256]{0:T(256)} %refs_2_.1) | copy-start | bytes 3076
  61.6 26.1 %copy-start.9 = (bf16[256,512]{1,0:T(8,128)(2,1)S(1)}, bf16[256,512]{1,0:T(8,128)(2,1)}, u32[]{:S(2)}) copy-start(bf16[256,512]{1,0:T(8,128)(2,1)} %param.19) | copy-start | bytes 786436

commit v3 on v2

--- a/solution.py
+++ b/solution.py
@@ -59,36 +59,40 @@
     return jnp.concatenate([out[i * rows : (i + 1) * rows] for i in range(last - first)], axis=1)
 
 
-def tail_kernel(value, key, gate_one, gate_two, taps, tails, matrices, mixed, one, two):
+def tail_kernel(value, key, gate, taps, tails, matrices):
     groups = taps.shape[0]
     rows = value.shape[0] // groups
-    width = mixed.shape[1]
     for g in range(groups):
         at = pl.ds(g * rows, rows)
         matrix = band(taps, g)
         matrices[g] = matrix
-        block = (key[at, :].astype(F32) * value[at, :].astype(F32)).astype(BF16)
-        tails[at, :LANES] = block[:, width:]
-        first = conv_blocks(block[:, width - LANES :], matrix, 0, 1)
-        tails[at, LANES:] = (gate_one[at, width:].astype(F32) * first).astype(BF16)
-        mixed[at, :] = block[:, :width]
-    one[...] = gate_one[:, :width]
-    two[...] = gate_two[...]
-
-
-def near_kernel(mixed, gate_one, gate_two, ahead, taps, tails, kept, out, matrices):
+        mixed = (key[at, :].astype(F32) * value[at, :].astype(F32)).astype(BF16)
+        tails[at, :LANES] = mixed[:, LANES:]
+        first = conv_blocks(mixed, matrix, 0, 1)
+        tails[at, LANES:] = (gate[at, :].astype(F32) * first).astype(BF16)
+
+
+def near_kernel(
+    value, key, gate_one, gate_two, ahead, taps, tails, kept, out, matrices, mixed, one, two
+):
     groups = taps.shape[0]
-    rows = mixed.shape[0] // groups
+    rows = value.shape[0] // groups
+    half = 2 * LANES
     for g in range(groups):
         at = pl.ds(g * rows, rows)
         matrix = band(taps, g)
         matrices[g] = matrix
-        first = conv_blocks(mixed[at, :], ahead[g], 0, 2)
-        first = (gate_one[at, LANES:].astype(F32) * first).astype(BF16)
+        block = key[at, : 3 * LANES].astype(F32) * value[at, : 3 * LANES].astype(F32)
+        block = block.astype(BF16)
+        mixed[at, :] = block[:, :LANES]
+        first = conv_blocks(block, ahead[g], 0, 2)
+        first = (gate_one[at, LANES : 3 * LANES].astype(F32) * first).astype(BF16)
         kept[at, :] = first[:, :LANES]
         first = jnp.concatenate([first, tails[at, LANES:]], axis=1)
         second = conv_blocks(first, matrix, 0, 2)
-        out[at, :] = (gate_two[at, 2 * LANES :].astype(F32) * second).astype(BF16)
+        out[at, :] = (gate_two[at, half:].astype(F32) * second).astype(BF16)
+    one[...] = gate_one[:, :LANES]
+    two[...] = gate_two[:, :half]
 
 
 def edge_kernel(mixed, gate_one, gate_two, kept, matrices_one, matrices_two, halo, *refs):
@@ -97,12 +101,12 @@
     rows = mixed.shape[0] // groups
     for g in range(groups):
         at = pl.ds(g * rows, rows)
-        first = jnp.concatenate([halo[at, :LANES], mixed[at, :LANES]], axis=1)
+        first = jnp.concatenate([halo[at, :LANES], mixed[at, :]], axis=1)
         first = conv_blocks(first, matrices_one[g], 0, 1)
-        first = (gate_one[at, :LANES].astype(F32) * first).astype(BF16)
+        first = (gate_one[at, :].astype(F32) * first).astype(BF16)
         first = jnp.concatenate([halo[at, LANES:], first, kept[at, :]], axis=1)
         second = conv_blocks(first, matrices_two[g], 0, 2)
-        out[at, : 2 * LANES] = (gate_two[at, : 2 * LANES].astype(F32) * second).astype(BF16)
+        out[at, : 2 * LANES] = (gate_two[at, :].astype(F32) * second).astype(BF16)
         if not SPLIT:
             out[at, 2 * LANES :] = refs[0][at, :]
 
@@ -217,36 +221,52 @@
     half = length // 2
     outer, outer_t, ahead, back, cos, sin = [near_core(t) for t in tables(length * devices, devices)]
     bands = pltpu.VMEM((groups, 2 * LANES, LANES), BF16)
-    width = length - LANES
-    tails, ones, mixed, gate_one, gate_two = call(
+    block = pltpu.VMEM((channels, LANES), BF16)
+    pair = pltpu.VMEM((channels, 2 * LANES), BF16)
+    value, key, gate_one, gate_two = map(in_hbm, (value_in, key_in, gate_first, gate_second))
+    tails, ones = call(
         tail_kernel,
-        (
-            pltpu.VMEM((channels, 2 * LANES), BF16),
-            bands,
-            pltpu.VMEM((channels, width), BF16),
-            pltpu.VMEM((channels, width), BF16),
-            pltpu.VMEM((channels, length), BF16),
-        ),
+        (pair, bands),
         "tail",
-        *map(in_hbm, (value_in, key_in, gate_first, gate_second, filter_first)),
+        value,
+        key,
+        gate_one,
+        in_hbm(filter_first),
+        specs=[
+            pl.BlockSpec((channels, half), lambda i: (0, 1)),
+            pl.BlockSpec((channels, half), lambda i: (0, 1)),
+            pl.BlockSpec((channels, LANES), lambda i: (0, length // LANES - 1)),
+            VMEM,
+        ],
     )
     halo = lax.ppermute(tails, "ctx", [(i, i + 1) for i in range(devices - 1)])
-    mixed, gate_one, gate_two, ones = map(near_core, (mixed, gate_one, gate_two, ones))
-    kept, late, twos = call(
+    ones = near_core(ones)
+    kept, late, twos, mixed, gate_one, gate_two = call(
         near_kernel,
-        (
-            pltpu.VMEM((channels, LANES), BF16),
-            pltpu.VMEM((channels, half), BF16),
-            bands,
-        ),
+        (block, pair, bands, block, block, pair),
         "near",
-        mixed,
+        value,
+        key,
         gate_one,
         gate_two,
         ones,
-        near_core(filter_second),
+        in_hbm(filter_second),
         near_core(tails),
     )
+    plane = pltpu.VMEM((length // LANES, devices * per, LANES), F32)
+    spectrum = call(
+        filter_kernel,
+        pltpu.VMEM((per, LANES, 2 * LANES), F32),
+        "spectrum",
+        near_core(long_filter),
+        outer,
+        ahead,
+        cos,
+        sin,
+        scratch=[plane],
+    )
+    kept, spectrum = lax.optimization_barrier((kept, spectrum))
+    mixed, gate_one, gate_two = map(near_core, (mixed, gate_one, gate_two))
     width = half if SPLIT else length
     rest = () if SPLIT else (near_core(late),)
     early = call(
@@ -261,18 +281,6 @@
         near_core(twos),
         near_core(halo),
         *rest,
-    )
-    plane = pltpu.VMEM((length // LANES, devices * per, LANES), F32)
-    spectrum = call(
-        filter_kernel,
-        pltpu.VMEM((per, LANES, 2 * LANES), F32),
-        "spectrum",
-        near_core(long_filter),
-        outer,
-        ahead,
-        cos,
-        sin,
-        scratch=[plane],
     )
 
     def swap(data):

time: 88.8 us -> 87.4 us (0.984)
  the two profiles are of different devices: /device:TPU:65 before, /device:TPU:105 now
where the time goes in v3:
time: 87.4 us; the launch traced here: 87.2 us
  blocking collectives  76.1 us (87%)
  Pallas kernels  6.33 us (7%)
  starting transfers between devices  3.68 us (4%)
    all_to_all x2, blocking collectives, swap(): return lax.all_to_all(data, 'ctx', split_axis=0, concat_axis=0, tiled=True)  76.1 us
    pallas_call x5, Pallas kernels, call(): pl.pallas_call(kernel, out_shape=outs, grid=(1,), in_specs=specs or [VMEM...  6.33 us
    ppermute x1, starting transfers between devices, shards(): halo = lax.ppermute(tails, 'ctx', [(i, i + 1) for i in range(devices - 1)])  3.68 us
  transfers between devices with their start and end apart: 1, of which 0 were waited for; matrix products, arithmetic and copies ran while one was open for 0% of the time, Pallas kernels for 3%

profile of v3, /device:TPU:105, one launch (start us, length us, event | category | flops | bytes accessed | tf_op | source)
XLA Modules:
  0.0 87.2 jit_solution(7343175568880665828)
XLA Ops:
  0.0 1.8 %tail.1 = (bf16[256,256]{1,0:T(8,128)(2,1)S(1)}, bf16[16,256,128]{2,1,0:T(8,128)(2,1)S(1)}) custom-call(bf16[256,512]{1,0:T(8,128)(2,1)} %value.3, bf16[256,512]{1,0:T(8,128)(2,1)} %key.3, bf16[256,512]{1,0:T(8,128)(2,1)} %gate_one.1, bf16[16,128]{1,0:T(8,128)(2,1)} %taps.3), custom_call_target="tpu_custom_call" | custom-call | tf_op jit(solution)/shard_map/tail/pallas_call | solution.py:26
  1.8 3.7 %collective-permute-start = (bf16[256,256]{1,0:T(8,128)(2,1)S(1)}, bf16[256,256]{1,0:T(8,128)(2,1)S(1)}, u32[]{:S(2)}, u32[]{:S(2)}) collective-permute-start(bf16[256,256]{1,0:T(8,128)(2,1)S(1)} %get-tuple-element.16.tails), channel_id=1, source_target_pairs={{0,32},{32,64},{64,96},{96,128},{128,160},{160,192},{192,224},{224... | collective-permute-start | bytes 393224 | tf_op jit(solution)/shard_map/ppermute | solution.py:242
  5.5 0.0 copy-start
  5.5 0.0 copy-start.1
  5.5 0.0 copy-start.2
  5.5 0.0 copy-start.3
  5.5 0.0 copy-start.4
  5.5 2.0 %near.1 = (bf16[256,128]{1,0:T(8,128)(2,1)S(1)}, bf16[256,256]{1,0:T(8,128)(2,1)S(1)}, bf16[16,256,128]{2,1,0:T(8,128)(2,1)S(1)}, bf16[256,128]{1,0:T(8,128)(2,1...) custom-call(bf16[256,512]{1,0:T(8,128)(2,1)} %value.3, bf16[256,512]{1,0:T(8,128)(2,1)} %key.3, ...), custom_call_target="tpu_custom_call" | custom-call | tf_op jit(solution)/shard_map/near/pallas_call | solution.py:26
  7.5 0.0 copy-done
  7.5 0.0 copy-done.1
  7.5 0.0 copy-done.2
  7.6 0.0 copy-done.3
  7.6 0.0 copy-done.4
  7.6 0.5 spectrum.1.refs_1_
  8.1 0.0 collective-permute-done.halo
  8.1 0.5 edge.1
  8.6 0.0 copy-start.5
  8.7 0.0 copy-start.6
  8.7 0.0 copy-start.7
  8.7 50.1 %all_to_all.10.refs_0_ = bf16[32,8,512]{2,1,0:T(8,128)(2,1)S(1)} all-to-all(bf16[32,8,512]{2,1,0:T(8,128)(2,1)S(1)} %bitcast.4), channel_id=1, replica_groups=mesh['ctx'=32,'ch'=32] {'ctx'}, dimensions={0} | all-to-all | bytes 524288 | tf_op jit(solution)/shard_map/all_to_all | solution.py:287
  58.7 0.0 copy-done.5
  58.7 0.0 copy-done.6
  58.7 0.0 copy-done.7
  58.7 1.5 %long.1 = bf16[32,8,512]{2,1,0:T(8,128)(2,1)S(1)} custom-call(bf16[32,8,512]{2,1,0:T(8,128)(2,1)S(1)} %all_to_all.10.refs_0_, f32[8,128,256]{2,1,0:T(8,128)S(1)} %spectrum.1.refs_1_, f32[256]{0:T(256)S(1)} %copy-done.7, bf16[256,128]{1,0:T(8,128)(2,1)S(1)} %copy-done.2, bf16[128,256]{1,0:T(8,128)(2,1)S(1)} %copy-done.6, bf16[256,256]{1,0:T(8,128)(2,1)S(1)} %copy-done, ...), custom_call_target="tpu_custom_call" | custom-call | tf_op jit(solution)/shard_map/long/pallas_call | solution.py:26
  60.3 0.0 copy-start.8
  60.3 26.1 %all_to_all.11 = bf16[32,8,512]{2,1,0:T(8,128)(2,1)S(1)} all-to-all(bf16[32,8,512]{2,1,0:T(8,128)(2,1)S(1)} %long.1), channel_id=1, replica_groups=mesh['ctx'=32,'ch'=32] {'ctx'}, dimensions={0} | all-to-all | bytes 524288 | tf_op jit(solution)/shard_map/all_to_all | solution.py:287
  86.4 0.0 copy-done.8
  86.4 0.8 fusion
Async XLA Ops:
  1.8 6.3 %collective-permute-start = (bf16[256,256]{1,0:T(8,128)(2,1)S(1)}, bf16[256,256]{1,0:T(8,128)(2,1)S(1)}, u32[]{:S(2)}, u32[]{:S(2)}) collective-permute-start(bf16[256,256]{1,0:T(8,128)(2,1)S(1)} %get-tuple-element.16.tails), channel_id=1, source_target_pairs={{0,32},{32,64},{64,96},{96,128},{128,160},{160,192},{192,224},{224... | collective-permute-start | bytes 393224 | tf_op jit(solution)/shard_map/ppermute | solution.py:242
  5.5 2.0 %copy-start = (bf16[256,256]{1,0:T(8,128)(2,1)S(1)}, bf16[256,256]{1,0:T(8,128)(2,1)}, u32[]{:S(2)}) copy-start(bf16[256,256]{1,0:T(8,128)(2,1)} %constant.22.ahead.refs_5_) | copy-start | bytes 393220
  5.5 2.0 %copy-start.1 = (bf16[8,16384]{1,0:T(8,128)(2,1)S(1)}, bf16[8,16384]{1,0:T(8,128)(2,1)}, u32[]{:S(2)}) copy-start(bf16[8,16384]{1,0:T(8,128)(2,1)} %taps.5) | copy-start | bytes 786436
  5.5 2.0 %copy-start.2 = (bf16[256,128]{1,0:T(8,128)(2,1)S(1)}, bf16[256,128]{1,0:T(8,128)(2,1)}, u32[]{:S(2)}) copy-start(bf16[256,128]{1,0:T(8,128)(2,1)} %constant.21.outer.refs_3_) | copy-start | bytes 196612
  5.5 2.0 %copy-start.3 = (f32[128,128]{1,0:T(8,128)S(1)}, f32[128,128]{1,0:T(8,128)}, u32[]{:S(2)}) copy-start(f32[128,128]{1,0:T(8,128)} %constant.17.clone.sin.refs_8_) | copy-start | bytes 196612
  5.5 2.0 %copy-start.4 = (f32[128,128]{1,0:T(8,128)S(1)}, f32[128,128]{1,0:T(8,128)}, u32[]{:S(2)}) copy-start(f32[128,128]{1,0:T(8,128)} %constant.16.clone.cos.refs_7_) | copy-start | bytes 196612
  8.6 50.1 %copy-start.5 = (bf16[256,256]{1,0:T(8,128)(2,1)S(1)}, bf16[256,256]{1,0:T(8,128)(2,1)}, u32[]{:S(2)}) copy-start(bf16[256,256]{1,0:T(8,128)(2,1)} %constant.24.refs_6_) | copy-start | bytes 393220
  8.7 50.1 %copy-start.6 = (bf16[128,256]{1,0:T(8,128)(2,1)S(1)}, bf16[128,256]{1,0:T(8,128)(2,1)}, u32[]{:S(2)}) copy-start(bf16[128,256]{1,0:T(8,128)(2,1)} %constant.23.refs_4_) | copy-start | bytes 196612
  8.7 50.1 %copy-start.7 = (f32[256]{0:T(256)S(1)}, f32[256]{0:T(256)}, u32[]{:S(2)}) copy-start(f32[256]{0:T(256)} %refs_2_.1) | copy-start | bytes 3076
  60.3 26.1 %copy-start.8 = (bf16[256,512]{1,0:T(8,128)(2,1)S(1)}, bf16[256,512]{1,0:T(8,128)(2,1)}, u32[]{:S(2)}) copy-start(bf16[256,512]{1,0:T(8,128)(2,1)} %param.19) | copy-start | bytes 786436

commit v4 on v3

--- a/solution.py
+++ b/solution.py
@@ -6,8 +6,11 @@
 from jax.experimental.pallas import tpu as pltpu
 from jax.sharding import PartitionSpec as P
 
+
 SPLIT = False
 LANES = 128
+ROW = 8
+PARTS = 4
 VMEM = pl.BlockSpec(memory_space=pltpu.VMEM)
 SMEM = pl.BlockSpec(memory_space=pltpu.SMEM)
 BF16 = jnp.bfloat16
@@ -22,7 +25,7 @@
     return pltpu.with_memory_space_constraint(data, pltpu.HBM)
 
 
-def call(kernel, outs, name, *args, specs=None, scratch=()):
+def call(kernel, outs, *args, specs=None, scratch=()):
     return pl.pallas_call(
         kernel,
         out_shape=outs,
@@ -31,7 +34,6 @@
         out_specs=(VMEM,) * len(outs) if isinstance(outs, tuple) else VMEM,
         scratch_shapes=list(scratch),
         compiler_params=pltpu.CompilerParams(vmem_limit_bytes=16 << 20),
-        name=name,
     )(*args)
 
 
@@ -95,16 +97,17 @@
     two[...] = gate_two[:, :half]
 
 
-def edge_kernel(mixed, gate_one, gate_two, kept, matrices_one, matrices_two, halo, *refs):
+def edge_kernel(mixed, gate_one, gate_two, kept, matrices_one, matrices_two, far, close, *refs):
     out = refs[-1]
     groups = matrices_one.shape[0]
     rows = mixed.shape[0] // groups
     for g in range(groups):
         at = pl.ds(g * rows, rows)
-        first = jnp.concatenate([halo[at, :LANES], mixed[at, :]], axis=1)
+        halo = far[at, :] + close[at, :]
+        first = jnp.concatenate([halo[:, :LANES], mixed[at, :]], axis=1)
         first = conv_blocks(first, matrices_one[g], 0, 1)
         first = (gate_one[at, :].astype(F32) * first).astype(BF16)
-        first = jnp.concatenate([halo[at, LANES:], first, kept[at, :]], axis=1)
+        first = jnp.concatenate([halo[:, LANES:], first, kept[at, :]], axis=1)
         second = conv_blocks(first, matrices_two[g], 0, 2)
         out[at, : 2 * LANES] = (gate_two[at, :].astype(F32) * second).astype(BF16)
         if not SPLIT:
@@ -203,6 +206,18 @@
         out[:, :, q * n : (q + 1) * n] = block.astype(BF16)
 
 
+def gate_kernel(gate, data, out, held, sems):
+    rows = gate.shape[0] // PARTS
+    copies = []
+    for p in range(PARTS):
+        at = pl.ds(p * rows, rows)
+        held[p] = (gate[at, :].astype(F32) * data[at, :].astype(F32)).astype(BF16)
+        copies.append(pltpu.make_async_copy(held.at[p], out.at[at, :], sems.at[p]))
+        copies[-1].start()
+    for copy in copies:
+        copy.wait()
+
+
 def shards(
     value_in,
     key_in,
@@ -227,7 +242,6 @@
     tails, ones = call(
         tail_kernel,
         (pair, bands),
-        "tail",
         value,
         key,
         gate_one,
@@ -239,12 +253,13 @@
             VMEM,
         ],
     )
-    halo = lax.ppermute(tails, "ctx", [(i, i + 1) for i in range(devices - 1)])
+    pairs = [(i, i + 1) for i in range(devices - 1)]
+    far = lax.ppermute(tails, "ctx", [p for p in pairs if p[1] % ROW == 0])
+    close = lax.ppermute(tails, "ctx", [p for p in pairs if p[1] % ROW])
     ones = near_core(ones)
     kept, late, twos, mixed, gate_one, gate_two = call(
         near_kernel,
         (block, pair, bands, block, block, pair),
-        "near",
         value,
         key,
         gate_one,
@@ -257,7 +272,6 @@
     spectrum = call(
         filter_kernel,
         pltpu.VMEM((per, LANES, 2 * LANES), F32),
-        "spectrum",
         near_core(long_filter),
         outer,
         ahead,
@@ -272,14 +286,14 @@
     early = call(
         edge_kernel,
         pltpu.VMEM((channels, width), BF16),
-        "edge",
         mixed,
         gate_one,
         gate_two,
         near_core(kept),
         ones,
         near_core(twos),
-        near_core(halo),
+        near_core(far),
+        near_core(close),
         *rest,
     )
 
@@ -292,7 +306,6 @@
     long_out = call(
         long_kernel,
         pltpu.VMEM((devices, per, length), BF16),
-        "long",
         *map(near_core, moved),
         near_core(spectrum),
         skip_gain,
@@ -306,7 +319,18 @@
         scratch=[plane, plane],
     )
     back_home = swap(long_out).reshape(channels, length)
-    return (gate_long.astype(F32) * back_home.astype(F32)).astype(BF16)
+    return pl.pallas_call(
+        gate_kernel,
+        out_shape=jax.ShapeDtypeStruct((channels, length), BF16),
+        in_specs=[VMEM, VMEM],
+        out_specs=pl.BlockSpec(memory_space=pl.ANY),
+        scratch_shapes=[
+            pltpu.VMEM((PARTS, channels // PARTS, length), BF16),
+            pltpu.SemaphoreType.DMA((PARTS,)),
+        ],
+        compiler_params=pltpu.CompilerParams(vmem_limit_bytes=16 << 20),
+        name="gate",
+    )(near_core(gate_long), near_core(back_home))
 
 
 def solution(mesh):

time: 87.4 us -> 89.1 us (1.019)
  the two profiles are of different devices: /device:TPU:105 before, /device:TPU:65 now
where the time goes in v4:
time: 89.1 us; the launch traced here: 88.9 us
  blocking collectives  77.2 us (87%)
  Pallas kernels  7.08 us (8%)
  starting transfers between devices  4.35 us (5%)
    all_to_all x2, blocking collectives, swap(): return lax.all_to_all(data, 'ctx', split_axis=0, concat_axis=0, tiled=True)  77.2 us
    pallas_call x5, Pallas kernels, call(): pl.pallas_call(kernel, out_shape=outs, grid=(1,), in_specs=specs or [VMEM...  6.33 us
    ppermute x1, starting transfers between devices, shards(): close = lax.ppermute(tails, 'ctx', [p for p in pairs if p[1] % ROW])  3.68 us
  transfers between devices with their start and end apart: 2, of which 0 were waited for; matrix products, arithmetic and copies ran while one was open for 0% of the time, Pallas kernels for 3%

profile of v4, /device:TPU:65, one launch (start us, length us, event | category | flops | bytes accessed | tf_op | source)
XLA Modules:
  0.0 88.9 jit_solution(2143592745160530921)
XLA Ops:
  0.0 1.8 %shard_map.145 = (bf16[256,256]{1,0:T(8,128)(2,1)S(1)}, bf16[16,256,128]{2,1,0:T(8,128)(2,1)S(1)}) custom-call(bf16[256,512]{1,0:T(8,128)(2,1)} %value.3, bf16[256,512]{1,0:T(8,128)(2,1)} %key.3, bf16[256,512]{1,0:T(8,128)(2,1)} %gate_one.1, bf16[16,128]{1,0:T(8,128)(2,1)} %taps.3), custom_call_target="tpu_custom_call" | custom-call | tf_op jit(solution)/shard_map/pallas_call | solution.py:29
  1.8 3.7 %collective-permute-start.1 = (bf16[256,256]{1,0:T(8,128)(2,1)S(1)}, bf16[256,256]{1,0:T(8,128)(2,1)S(1)}, u32[]{:S(2)}, u32[]{:S(2)}) collective-permute-start(bf16[256,256]{1,0:T(8,128)(2,1)S(1)} %get-tuple-element.16.tails), channel_id=1, source_target_pairs={{0,32},{32,64},{64,96},{96,128},{128,160},{160,192},{192,224},{256... | collective-permute-start | bytes 393224 | tf_op jit(solution)/shard_map/ppermute | solution.py:258
  5.5 0.7 collective-permute-start
  6.2 0.0 copy-start
  6.2 0.0 copy-start.1
  6.2 0.0 copy-start.3
  6.2 0.0 copy-start.4
  6.2 0.0 copy-start.5
  6.2 2.0 %shard_map.146 = (bf16[256,128]{1,0:T(8,128)(2,1)S(1)}, bf16[256,256]{1,0:T(8,128)(2,1)S(1)}, bf16[16,256,128]{2,1,0:T(8,128)(2,1)S(1)}, bf16[256,128]{1,0:T(8,1...) custom-call(bf16[256,512]{1,0:T(8,128)(2,1)} %value.3, bf16[256,512]{1,0:T(8,128)(2,1)} %key.3, ...), custom_call_target="tpu_custom_call" | custom-call | tf_op jit(solution)/shard_map/pallas_call | solution.py:29
  8.2 0.0 copy-done
  8.2 0.0 copy-done.1
  8.2 0.0 copy-done.3
  8.2 0.0 copy-done.4
  8.2 0.0 copy-done.5
  8.3 0.5 shard_map.147.refs_1_
  8.8 0.0 collective-permute-done.1.close
  8.8 0.0 collective-permute-done.far
  8.8 0.5 shard_map.148
  9.3 0.0 copy-start.6
  9.3 0.0 copy-start.7
  9.4 0.0 copy-start.8
  9.4 51.1 %all_to_all.10.refs_0_ = bf16[32,8,512]{2,1,0:T(8,128)(2,1)S(1)} all-to-all(bf16[32,8,512]{2,1,0:T(8,128)(2,1)S(1)} %bitcast.2), channel_id=1, replica_groups=mesh['ctx'=32,'ch'=32] {'ctx'}, dimensions={0} | all-to-all | bytes 524288 | tf_op jit(solution)/shard_map/all_to_all | solution.py:301
  60.5 0.0 copy-done.6
  60.5 0.0 copy-done.7
  60.5 0.0 copy-done.8
  60.5 1.5 %shard_map.149 = bf16[32,8,512]{2,1,0:T(8,128)(2,1)S(1)} custom-call(bf16[32,8,512]{2,1,0:T(8,128)(2,1)S(1)} %all_to_all.10.refs_0_, f32[8,128,256]{2,1,0:T(8,128)S(1)} %shard_map.147.refs_1_, f32[256]{0:T(256)S(1)} %copy-done.8, bf16[256,128]{1,0:T(8,128)(2,1)S(1)} %copy-done.3, bf16[128,256]{1,0:T(8,128)(2,1)S(1)} %copy-done.7, ...), custom_call_target="tpu_custom_call" | custom-call | tf_op jit(solution)/shard_map/pallas_call | solution.py:29
  62.0 0.0 copy-start.2
  62.0 26.1 %all_to_all.11 = bf16[32,8,512]{2,1,0:T(8,128)(2,1)S(1)} all-to-all(bf16[32,8,512]{2,1,0:T(8,128)(2,1)S(1)} %shard_map.149), channel_id=1, replica_groups=mesh['ctx'=32,'ch'=32] {'ctx'}, dimensions={0} | all-to-all | bytes 524288 | tf_op jit(solution)/shard_map/all_to_all | solution.py:301
  88.1 0.0 copy-done.2
  88.1 0.7 gate.4
Async XLA Ops:
  1.8 7.0 %collective-permute-start.1 = (bf16[256,256]{1,0:T(8,128)(2,1)S(1)}, bf16[256,256]{1,0:T(8,128)(2,1)S(1)}, u32[]{:S(2)}, u32[]{:S(2)}) collective-permute-start(bf16[256,256]{1,0:T(8,128)(2,1)S(1)} %get-tuple-element.16.tails), channel_id=1, source_target_pairs={{0,32},{32,64},{64,96},{96,128},{128,160},{160,192},{192,224},{256... | collective-permute-start | bytes 393224 | tf_op jit(solution)/shard_map/ppermute | solution.py:258
  5.5 3.3 %collective-permute-start = (bf16[256,256]{1,0:T(8,128)(2,1)S(1)}, bf16[256,256]{1,0:T(8,128)(2,1)S(1)}, u32[]{:S(2)}, u32[]{:S(2)}) collective-permute-start(bf16[256,256]{1,0:T(8,128)(2,1)S(1)} %get-tuple-element.16.tails), channel_id=1, source_target_pairs={{224,256},{480,512},{736,768},{225,257},{481,513},{737,769},{226,2... | collective-permute-start | bytes 393224 | tf_op jit(solution)/shard_map/ppermute | solution.py:257
  6.2 2.0 %copy-start = (bf16[256,256]{1,0:T(8,128)(2,1)S(1)}, bf16[256,256]{1,0:T(8,128)(2,1)}, u32[]{:S(2)}) copy-start(bf16[256,256]{1,0:T(8,128)(2,1)} %constant.22.ahead.refs_5_) | copy-start | bytes 393220
  6.2 2.0 %copy-start.1 = (bf16[8,16384]{1,0:T(8,128)(2,1)S(1)}, bf16[8,16384]{1,0:T(8,128)(2,1)}, u32[]{:S(2)}) copy-start(bf16[8,16384]{1,0:T(8,128)(2,1)} %taps.5) | copy-start | bytes 786436
  6.2 2.0 %copy-start.3 = (bf16[256,128]{1,0:T(8,128)(2,1)S(1)}, bf16[256,128]{1,0:T(8,128)(2,1)}, u32[]{:S(2)}) copy-start(bf16[256,128]{1,0:T(8,128)(2,1)} %constant.21.outer.refs_3_) | copy-start | bytes 196612
  6.2 2.0 %copy-start.4 = (f32[128,128]{1,0:T(8,128)S(1)}, f32[128,128]{1,0:T(8,128)}, u32[]{:S(2)}) copy-start(f32[128,128]{1,0:T(8,128)} %constant.17.clone.sin.refs_8_) | copy-start | bytes 196612
  6.2 2.0 %copy-start.5 = (f32[128,128]{1,0:T(8,128)S(1)}, f32[128,128]{1,0:T(8,128)}, u32[]{:S(2)}) copy-start(f32[128,128]{1,0:T(8,128)} %constant.16.clone.cos.refs_7_) | copy-start | bytes 196612
  9.3 51.2 %copy-start.6 = (bf16[256,256]{1,0:T(8,128)(2,1)S(1)}, bf16[256,256]{1,0:T(8,128)(2,1)}, u32[]{:S(2)}) copy-start(bf16[256,256]{1,0:T(8,128)(2,1)} %constant.24.refs_6_) | copy-start | bytes 393220
  9.3 51.1 %copy-start.7 = (bf16[128,256]{1,0:T(8,128)(2,1)S(1)}, bf16[128,256]{1,0:T(8,128)(2,1)}, u32[]{:S(2)}) copy-start(bf16[128,256]{1,0:T(8,128)(2,1)} %constant.23.refs_4_) | copy-start | bytes 196612
  9.4 51.1 %copy-start.8 = (f32[256]{0:T(256)S(1)}, f32[256]{0:T(256)}, u32[]{:S(2)}) copy-start(f32[256]{0:T(256)} %refs_2_.1) | copy-start | bytes 3076
  62.0 26.1 %copy-start.2 = (bf16[256,512]{1,0:T(8,128)(2,1)S(1)}, bf16[256,512]{1,0:T(8,128)(2,1)}, u32[]{:S(2)}) copy-start(bf16[256,512]{1,0:T(8,128)(2,1)} %gate.5) | copy-start | bytes 786436

commit v5 on v4

--- a/solution.py
+++ b/solution.py
@@ -11,6 +11,7 @@
 LANES = 128
 ROW = 8
 PARTS = 4
+BATCH = 2
 VMEM = pl.BlockSpec(memory_space=pltpu.VMEM)
 SMEM = pl.BlockSpec(memory_space=pltpu.SMEM)
 BF16 = jnp.bfloat16
@@ -61,17 +62,36 @@
     return jnp.concatenate([out[i * rows : (i + 1) * rows] for i in range(last - first)], axis=1)
 
 
-def tail_kernel(value, key, gate, taps, tails, matrices):
+def tail_kernel(value, key, gate, taps, tails, matrices, values, keys, gates, held, sems):
     groups = taps.shape[0]
-    rows = value.shape[0] // groups
+    rows, length = value.shape[0] // groups, value.shape[1]
+    width = values.shape[1]
+    copies = [
+        pltpu.make_async_copy(source, target, sems.at[i])
+        for i, (source, target) in enumerate(
+            (
+                (taps, held),
+                (value.at[:, pl.ds(length - width, width)], values),
+                (key.at[:, pl.ds(length - width, width)], keys),
+                (gate.at[:, pl.ds(length - LANES, LANES)], gates),
+            )
+        )
+    ]
+    for copy in copies:
+        copy.start()
+    copies[0].wait()
+    for g in range(groups // 2):
+        matrices[g] = band(held, g)
+    for copy in copies[1:]:
+        copy.wait()
     for g in range(groups):
         at = pl.ds(g * rows, rows)
-        matrix = band(taps, g)
-        matrices[g] = matrix
-        mixed = (key[at, :].astype(F32) * value[at, :].astype(F32)).astype(BF16)
+        if g >= groups // 2:
+            matrices[g] = band(held, g)
+        mixed = (keys[at, :].astype(F32) * values[at, :].astype(F32)).astype(BF16)
         tails[at, :LANES] = mixed[:, LANES:]
-        first = conv_blocks(mixed, matrix, 0, 1)
-        tails[at, LANES:] = (gate[at, :].astype(F32) * first).astype(BF16)
+        first = conv_blocks(mixed, matrices[g], 0, 1)
+        tails[at, LANES:] = (gates[at, :].astype(F32) * first).astype(BF16)
 
 
 def near_kernel(
@@ -144,15 +164,39 @@
     return jnp.concatenate(picked, axis=0)
 
 
-def transform(signals, outer, ahead, cos, sin):
-    n = LANES
-    parts = matmul(outer, jnp.concatenate([s.astype(BF16) for s in signals], axis=1))
+def side_by_side(signals):
+    return jnp.concatenate([s.astype(BF16) for s in signals], axis=1)
+
+
+def turn_ahead(parts, cos, sin):
+    n = LANES
     turned = []
-    for c in range(len(signals)):
-        re, im = parts[:n, c * n : (c + 1) * n], parts[n:, c * n : (c + 1) * n]
+    for at in range(0, parts.shape[1], n):
+        re, im = parts[:n, at : at + n], parts[n:, at : at + n]
         both = jnp.concatenate([re * cos + im * sin, im * cos - re * sin], axis=1)
         turned.append(both.astype(BF16))
-    return matmul(jnp.concatenate(turned, axis=0), ahead)
+    return jnp.concatenate(turned, axis=0)
+
+
+def weigh(waves, spectra):
+    n = LANES
+    products = []
+    for i, spectrum in enumerate(spectra):
+        re, im = waves[i * n : (i + 1) * n, :n], waves[i * n : (i + 1) * n, n:]
+        filter_re, filter_im = spectrum[:, :n], spectrum[:, n:]
+        both = [re * filter_re - im * filter_im, re * filter_im + im * filter_re]
+        products.append(jnp.concatenate(both, axis=1).astype(BF16))
+    return jnp.concatenate(products, axis=0)
+
+
+def turn_back(waves, cos, sin):
+    n = LANES
+    turned = []
+    for at in range(0, waves.shape[0], n):
+        re, im = waves[at : at + n, :n], waves[at : at + n, n:]
+        both = [re * cos - im * sin, re * sin + im * cos]
+        turned.append(jnp.concatenate(both, axis=0).astype(BF16))
+    return jnp.concatenate(turned, axis=1)
 
 
 def filter_kernel(taps, outer, ahead, cos, sin, spectrum, rows):
@@ -163,7 +207,8 @@
         at = pl.ds(b // per * channels, channels)
         rows[b % per, at, :] = taps[:, b * n : (b + 1) * n].astype(F32)
     signals = [gather_rows(rows, c, channels) for c in range(channels)]
-    waves = transform(signals, outer[...], ahead[...], cos[...], sin[...])
+    waves = matmul(outer[...], side_by_side(signals))
+    waves = matmul(turn_ahead(waves, cos[...], sin[...]), ahead[...])
     spectrum[...] = (waves * (1.0 / length)).reshape(spectrum.shape)
 
 
@@ -181,26 +226,21 @@
             rows[part * (width // n) + q] = flat[:, q * n : (q + 1) * n]
     base = lax.axis_index("ctx") * channels
     cosines, sines = cos[...], sin[...]
-    signals = [gather_rows(rows, c, channels) for c in range(channels)]
-    waves = transform(signals, outer[...], ahead[...], cosines, sines)
-    products = []
-    for c in range(channels):
-        re, im = waves[c * n : (c + 1) * n, :n], waves[c * n : (c + 1) * n, n:]
-        filter_re, filter_im = spectrum[c, :, :n], spectrum[c, :, n:]
-        both = [re * filter_re - im * filter_im, re * filter_im + im * filter_re]
-        products.append(jnp.concatenate(both, axis=1).astype(BF16))
-    waves = matmul(jnp.concatenate(products, axis=0), back[...])
-    turned = []
-    for c in range(channels):
-        re, im = waves[c * n : (c + 1) * n, :n], waves[c * n : (c + 1) * n, n:]
-        both = [re * cosines - im * sines, re * sines + im * cosines]
-        turned.append(jnp.concatenate(both, axis=0).astype(BF16))
-    results = matmul(outer_t[...], jnp.concatenate(turned, axis=1))
-    for c in range(channels):
-        result = results[:, c * n : (c + 1) * n] + skip[base + c] * signals[c]
-        for q in range(length // n):
-            at = pl.ds(c, devices, stride=channels)
-            outs[q, at, :] = result[q * devices : (q + 1) * devices]
+    batches = [range(c, c + BATCH) for c in range(0, channels, BATCH)]
+    signals = [[gather_rows(rows, c, channels) for c in batch] for batch in batches]
+    waves = [matmul(outer[...], side_by_side(s)) for s in signals]
+    waves = [matmul(turn_ahead(w, cosines, sines), ahead[...]) for w in waves]
+    waves = [
+        matmul(weigh(w, [spectrum[c] for c in batch]), back[...])
+        for w, batch in zip(waves, batches)
+    ]
+    waves = [matmul(outer_t[...], turn_back(w, cosines, sines)) for w in waves]
+    for batch, signal, result in zip(batches, signals, waves):
+        for i, c in enumerate(batch):
+            block = result[:, i * n : (i + 1) * n] + skip[base + c] * signal[i]
+            for q in range(length // n):
+                at = pl.ds(c, devices, stride=channels)
+                outs[q, at, :] = block[q * devices : (q + 1) * devices]
     for q in range(length // n):
         block = outs[q].reshape(devices, channels, n)
         out[:, :, q * n : (q + 1) * n] = block.astype(BF16)
@@ -246,11 +286,13 @@
         key,
         gate_one,
         in_hbm(filter_first),
-        specs=[
-            pl.BlockSpec((channels, half), lambda i: (0, 1)),
-            pl.BlockSpec((channels, half), lambda i: (0, 1)),
-            pl.BlockSpec((channels, LANES), lambda i: (0, length // LANES - 1)),
-            VMEM,
+        specs=[pl.BlockSpec(memory_space=pl.ANY)] * 4,
+        scratch=[
+            pair,
+            pair,
+            block,
+            pltpu.VMEM(filter_first.shape, BF16),
+            pltpu.SemaphoreType.DMA((4,)),
         ],
     )
     pairs = [(i, i + 1) for i in range(devices - 1)]

time: 89.1 us -> 88.9 us (level)
  the two profiles are of different devices: /device:TPU:65 before, /device:TPU:121 now
where the time goes in v5:
time: 88.9 us; the launch traced here: 88.7 us
  blocking collectives  77.2 us (87%)
  Pallas kernels  6.86 us (8%)
  starting transfers between devices  4.35 us (5%)
    all_to_all x2, blocking collectives, swap(): return lax.all_to_all(data, 'ctx', split_axis=0, concat_axis=0, tiled=True)  77.2 us
    pallas_call x5, Pallas kernels, call(): pl.pallas_call(kernel, out_shape=outs, grid=(1,), in_specs=specs or [VMEM...  6.11 us
    ppermute x1, starting transfers between devices, shards(): close = lax.ppermute(tails, 'ctx', [p for p in pairs if p[1] % ROW])  3.68 us
  transfers between devices with their start and end apart: 2, of which 0 were waited for; matrix products, arithmetic and copies ran while one was open for 0% of the time, Pallas kernels for 3%

profile of v5, /device:TPU:121, one launch (start us, length us, event | category | flops | bytes accessed | tf_op | source)
XLA Modules:
  0.0 88.7 jit_solution(11172426399973290004)
XLA Ops:
  0.0 1.6 %shard_map.145 = (bf16[256,256]{1,0:T(8,128)(2,1)S(1)}, bf16[16,256,128]{2,1,0:T(8,128)(2,1)S(1)}) custom-call(bf16[256,512]{1,0:T(8,128)(2,1)} %value.3, bf16[256,512]{1,0:T(8,128)(2,1)} %key.3, bf16[256,512]{1,0:T(8,128)(2,1)} %gate_one.1, bf16[16,128]{1,0:T(8,128)(2,1)} %taps.3), custom_call_target="tpu_custom_call" | custom-call | tf_op jit(solution)/shard_map/pallas_call | solution.py:30
  1.6 3.7 %collective-permute-start.1 = (bf16[256,256]{1,0:T(8,128)(2,1)S(1)}, bf16[256,256]{1,0:T(8,128)(2,1)S(1)}, u32[]{:S(2)}, u32[]{:S(2)}) collective-permute-start(bf16[256,256]{1,0:T(8,128)(2,1)S(1)} %get-tuple-element.16.tails), channel_id=1, source_target_pairs={{0,32},{32,64},{64,96},{96,128},{128,160},{160,192},{192,224},{256... | collective-permute-start | bytes 393224 | tf_op jit(solution)/shard_map/ppermute | solution.py:300
  5.3 0.7 collective-permute-start
  6.0 0.0 copy-start
  6.0 0.0 copy-start.1
  6.0 0.0 copy-start.3
  6.0 0.0 copy-start.4
  6.0 0.0 copy-start.5
  6.0 2.0 %shard_map.146 = (bf16[256,128]{1,0:T(8,128)(2,1)S(1)}, bf16[256,256]{1,0:T(8,128)(2,1)S(1)}, bf16[16,256,128]{2,1,0:T(8,128)(2,1)S(1)}, bf16[256,128]{1,0:T(8,1...) custom-call(bf16[256,512]{1,0:T(8,128)(2,1)} %value.3, bf16[256,512]{1,0:T(8,128)(2,1)} %key.3, ...), custom_call_target="tpu_custom_call" | custom-call | tf_op jit(solution)/shard_map/pallas_call | solution.py:30
  8.0 0.0 copy-done
  8.0 0.0 copy-done.1
  8.0 0.0 copy-done.3
  8.0 0.0 copy-done.4
  8.1 0.0 copy-done.5
  8.1 0.5 shard_map.147.refs_1_
  8.6 0.0 collective-permute-done.1.close
  8.6 0.0 collective-permute-done.far
  8.6 0.5 shard_map.148
  9.1 0.0 copy-start.6
  9.2 0.0 copy-start.7
  9.2 0.0 copy-start.8
  9.2 51.1 %all_to_all.10.refs_0_ = bf16[32,8,512]{2,1,0:T(8,128)(2,1)S(1)} all-to-all(bf16[32,8,512]{2,1,0:T(8,128)(2,1)S(1)} %bitcast.2), channel_id=1, replica_groups=mesh['ctx'=32,'ch'=32] {'ctx'}, dimensions={0} | all-to-all | bytes 524288 | tf_op jit(solution)/shard_map/all_to_all | solution.py:343
  60.3 0.0 copy-done.6
  60.3 0.0 copy-done.7
  60.3 0.0 copy-done.8
  60.3 1.5 %shard_map.149 = bf16[32,8,512]{2,1,0:T(8,128)(2,1)S(1)} custom-call(bf16[32,8,512]{2,1,0:T(8,128)(2,1)S(1)} %all_to_all.10.refs_0_, f32[8,128,256]{2,1,0:T(8,128)S(1)} %shard_map.147.refs_1_, f32[256]{0:T(256)S(1)} %copy-done.8, bf16[256,128]{1,0:T(8,128)(2,1)S(1)} %copy-done.3, bf16[128,256]{1,0:T(8,128)(2,1)S(1)} %copy-done.7, ...), custom_call_target="tpu_custom_call" | custom-call | tf_op jit(solution)/shard_map/pallas_call | solution.py:30
  61.8 0.0 copy-start.2
  61.8 26.1 %all_to_all.11 = bf16[32,8,512]{2,1,0:T(8,128)(2,1)S(1)} all-to-all(bf16[32,8,512]{2,1,0:T(8,128)(2,1)S(1)} %shard_map.149), channel_id=1, replica_groups=mesh['ctx'=32,'ch'=32] {'ctx'}, dimensions={0} | all-to-all | bytes 524288 | tf_op jit(solution)/shard_map/all_to_all | solution.py:343
  87.9 0.0 copy-done.2
  87.9 0.7 gate.4
Async XLA Ops:
  1.6 7.0 %collective-permute-start.1 = (bf16[256,256]{1,0:T(8,128)(2,1)S(1)}, bf16[256,256]{1,0:T(8,128)(2,1)S(1)}, u32[]{:S(2)}, u32[]{:S(2)}) collective-permute-start(bf16[256,256]{1,0:T(8,128)(2,1)S(1)} %get-tuple-element.16.tails), channel_id=1, source_target_pairs={{0,32},{32,64},{64,96},{96,128},{128,160},{160,192},{192,224},{256... | collective-permute-start | bytes 393224 | tf_op jit(solution)/shard_map/ppermute | solution.py:300
  5.3 3.3 %collective-permute-start = (bf16[256,256]{1,0:T(8,128)(2,1)S(1)}, bf16[256,256]{1,0:T(8,128)(2,1)S(1)}, u32[]{:S(2)}, u32[]{:S(2)}) collective-permute-start(bf16[256,256]{1,0:T(8,128)(2,1)S(1)} %get-tuple-element.16.tails), channel_id=1, source_target_pairs={{224,256},{480,512},{736,768},{225,257},{481,513},{737,769},{226,2... | collective-permute-start | bytes 393224 | tf_op jit(solution)/shard_map/ppermute | solution.py:299
  6.0 2.0 %copy-start = (bf16[256,256]{1,0:T(8,128)(2,1)S(1)}, bf16[256,256]{1,0:T(8,128)(2,1)}, u32[]{:S(2)}) copy-start(bf16[256,256]{1,0:T(8,128)(2,1)} %constant.22.ahead.refs_5_) | copy-start | bytes 393220
  6.0 2.0 %copy-start.1 = (bf16[8,16384]{1,0:T(8,128)(2,1)S(1)}, bf16[8,16384]{1,0:T(8,128)(2,1)}, u32[]{:S(2)}) copy-start(bf16[8,16384]{1,0:T(8,128)(2,1)} %taps.5) | copy-start | bytes 786436
  6.0 2.0 %copy-start.3 = (bf16[256,128]{1,0:T(8,128)(2,1)S(1)}, bf16[256,128]{1,0:T(8,128)(2,1)}, u32[]{:S(2)}) copy-start(bf16[256,128]{1,0:T(8,128)(2,1)} %constant.21.outer.refs_3_) | copy-start | bytes 196612
  6.0 2.0 %copy-start.4 = (f32[128,128]{1,0:T(8,128)S(1)}, f32[128,128]{1,0:T(8,128)}, u32[]{:S(2)}) copy-start(f32[128,128]{1,0:T(8,128)} %constant.17.clone.sin.refs_8_) | copy-start | bytes 196612
  6.0 2.0 %copy-start.5 = (f32[128,128]{1,0:T(8,128)S(1)}, f32[128,128]{1,0:T(8,128)}, u32[]{:S(2)}) copy-start(f32[128,128]{1,0:T(8,128)} %constant.16.clone.cos.refs_7_) | copy-start | bytes 196612
  9.1 51.2 %copy-start.6 = (bf16[256,256]{1,0:T(8,128)(2,1)S(1)}, bf16[256,256]{1,0:T(8,128)(2,1)}, u32[]{:S(2)}) copy-start(bf16[256,256]{1,0:T(8,128)(2,1)} %constant.24.refs_6_) | copy-start | bytes 393220
  9.2 51.1 %copy-start.7 = (bf16[128,256]{1,0:T(8,128)(2,1)S(1)}, bf16[128,256]{1,0:T(8,128)(2,1)}, u32[]{:S(2)}) copy-start(bf16[128,256]{1,0:T(8,128)(2,1)} %constant.23.refs_4_) | copy-start | bytes 196612
  9.2 51.1 %copy-start.8 = (f32[256]{0:T(256)S(1)}, f32[256]{0:T(256)}, u32[]{:S(2)}) copy-start(f32[256]{0:T(256)} %refs_2_.1) | copy-start | bytes 3076
  61.8 26.1 %copy-start.2 = (bf16[256,512]{1,0:T(8,128)(2,1)S(1)}, bf16[256,512]{1,0:T(8,128)(2,1)}, u32[]{:S(2)}) copy-start(bf16[256,512]{1,0:T(8,128)(2,1)} %gate.5) | copy-start | bytes 786436

commit v6 on v5

--- a/solution.py
+++ b/solution.py
@@ -10,8 +10,8 @@
 SPLIT = False
 LANES = 128
 ROW = 8
-PARTS = 4
-BATCH = 2
+PARTS = 2
+BATCH = 1
 VMEM = pl.BlockSpec(memory_space=pltpu.VMEM)
 SMEM = pl.BlockSpec(memory_space=pltpu.SMEM)
 BF16 = jnp.bfloat16
@@ -121,14 +121,20 @@
     out = refs[-1]
     groups = matrices_one.shape[0]
     rows = mixed.shape[0] // groups
-    for g in range(groups):
-        at = pl.ds(g * rows, rows)
-        halo = far[at, :] + close[at, :]
-        first = jnp.concatenate([halo[:, :LANES], mixed[at, :]], axis=1)
-        first = conv_blocks(first, matrices_one[g], 0, 1)
-        first = (gate_one[at, :].astype(F32) * first).astype(BF16)
-        first = jnp.concatenate([halo[:, LANES:], first, kept[at, :]], axis=1)
-        second = conv_blocks(first, matrices_two[g], 0, 2)
+    places = [pl.ds(g * rows, rows) for g in range(groups)]
+    halos = [far[at, :] + close[at, :] for at in places]
+    firsts = [
+        conv_blocks(
+            jnp.concatenate([halo[:, :LANES], mixed[at, :]], axis=1), matrices_one[g], 0, 1
+        )
+        for g, (at, halo) in enumerate(zip(places, halos))
+    ]
+    firsts = [
+        (gate_one[at, :].astype(F32) * first).astype(BF16) for at, first in zip(places, firsts)
+    ]
+    for g, (at, halo, first) in enumerate(zip(places, halos, firsts)):
+        wide = jnp.concatenate([halo[:, LANES:], first, kept[at, :]], axis=1)
+        second = conv_blocks(wide, matrices_two[g], 0, 2)
         out[at, : 2 * LANES] = (gate_two[at, :].astype(F32) * second).astype(BF16)
         if not SPLIT:
             out[at, 2 * LANES :] = refs[0][at, :]

time: 88.9 us -> 88.7 us (level)
  the two profiles are of different devices: /device:TPU:121 before, /device:TPU:65 now
where the time goes in v6:
time: 88.7 us; the launch traced here: 88.5 us
  blocking collectives  77.2 us (87%)
  Pallas kernels  6.67 us (8%)
  starting transfers between devices  4.35 us (5%)
    all_to_all x2, blocking collectives, swap(): return lax.all_to_all(data, 'ctx', split_axis=0, concat_axis=0, tiled=True)  77.2 us
    pallas_call x5, Pallas kernels, call(): pl.pallas_call(kernel, out_shape=outs, grid=(1,), in_specs=specs or [VMEM...  5.93 us
    ppermute x1, starting transfers between devices, shards(): close = lax.ppermute(tails, 'ctx', [p for p in pairs if p[1] % ROW])  3.68 us
  transfers between devices with their start and end apart: 2, of which 0 were waited for; matrix products, arithmetic and copies ran while one was open for 0% of the time, Pallas kernels for 3%

profile of v6, /device:TPU:65, one launch (start us, length us, event | category | flops | bytes accessed | tf_op | source)
XLA Modules:
  0.0 88.5 jit_solution(4137244965407197172)
XLA Ops:
  0.0 1.6 %shard_map.145 = (bf16[256,256]{1,0:T(8,128)(2,1)S(1)}, bf16[16,256,128]{2,1,0:T(8,128)(2,1)S(1)}) custom-call(bf16[256,512]{1,0:T(8,128)(2,1)} %value.3, bf16[256,512]{1,0:T(8,128)(2,1)} %key.3, bf16[256,512]{1,0:T(8,128)(2,1)} %gate_one.1, bf16[16,128]{1,0:T(8,128)(2,1)} %taps.3), custom_call_target="tpu_custom_call" | custom-call | tf_op jit(solution)/shard_map/pallas_call | solution.py:30
  1.6 3.7 %collective-permute-start.1 = (bf16[256,256]{1,0:T(8,128)(2,1)S(1)}, bf16[256,256]{1,0:T(8,128)(2,1)S(1)}, u32[]{:S(2)}, u32[]{:S(2)}) collective-permute-start(bf16[256,256]{1,0:T(8,128)(2,1)S(1)} %get-tuple-element.16.tails), channel_id=1, source_target_pairs={{0,32},{32,64},{64,96},{96,128},{128,160},{160,192},{192,224},{256... | collective-permute-start | bytes 393224 | tf_op jit(solution)/shard_map/ppermute | solution.py:306
  5.3 0.7 collective-permute-start
  6.0 0.0 copy-start
  6.0 0.0 copy-start.1
  6.0 0.0 copy-start.3
  6.0 0.0 copy-start.4
  6.0 0.0 copy-start.5
  6.0 2.0 %shard_map.146 = (bf16[256,128]{1,0:T(8,128)(2,1)S(1)}, bf16[256,256]{1,0:T(8,128)(2,1)S(1)}, bf16[16,256,128]{2,1,0:T(8,128)(2,1)S(1)}, bf16[256,128]{1,0:T(8,1...) custom-call(bf16[256,512]{1,0:T(8,128)(2,1)} %value.3, bf16[256,512]{1,0:T(8,128)(2,1)} %key.3, ...), custom_call_target="tpu_custom_call" | custom-call | tf_op jit(solution)/shard_map/pallas_call | solution.py:30
  8.0 0.0 copy-done
  8.0 0.0 copy-done.1
  8.0 0.0 copy-done.3
  8.0 0.0 copy-done.4
  8.1 0.0 copy-done.5
  8.1 0.5 shard_map.147.refs_1_
  8.6 0.0 collective-permute-done.1.close
  8.6 0.0 collective-permute-done.far
  8.6 0.4 shard_map.148
  9.1 0.0 copy-start.6
  9.1 0.0 copy-start.7
  9.1 0.0 copy-start.8
  9.1 51.1 %all_to_all.10.refs_0_ = bf16[32,8,512]{2,1,0:T(8,128)(2,1)S(1)} all-to-all(bf16[32,8,512]{2,1,0:T(8,128)(2,1)S(1)} %bitcast.2), channel_id=1, replica_groups=mesh['ctx'=32,'ch'=32] {'ctx'}, dimensions={0} | all-to-all | bytes 524288 | tf_op jit(solution)/shard_map/all_to_all | solution.py:349
  60.2 0.0 copy-done.6
  60.2 0.0 copy-done.7
  60.2 0.0 copy-done.8
  60.2 1.4 %shard_map.149 = bf16[32,8,512]{2,1,0:T(8,128)(2,1)S(1)} custom-call(bf16[32,8,512]{2,1,0:T(8,128)(2,1)S(1)} %all_to_all.10.refs_0_, f32[8,128,256]{2,1,0:T(8,128)S(1)} %shard_map.147.refs_1_, f32[256]{0:T(256)S(1)} %copy-done.8, bf16[256,128]{1,0:T(8,128)(2,1)S(1)} %copy-done.3, bf16[128,256]{1,0:T(8,128)(2,1)S(1)} %copy-done.7, ...), custom_call_target="tpu_custom_call" | custom-call | tf_op jit(solution)/shard_map/pallas_call | solution.py:30
  61.6 0.0 copy-start.2
  61.6 26.1 %all_to_all.11 = bf16[32,8,512]{2,1,0:T(8,128)(2,1)S(1)} all-to-all(bf16[32,8,512]{2,1,0:T(8,128)(2,1)S(1)} %shard_map.149), channel_id=1, replica_groups=mesh['ctx'=32,'ch'=32] {'ctx'}, dimensions={0} | all-to-all | bytes 524288 | tf_op jit(solution)/shard_map/all_to_all | solution.py:349
  87.7 0.0 copy-done.2
  87.7 0.7 gate.4
Async XLA Ops:
  1.6 7.0 %collective-permute-start.1 = (bf16[256,256]{1,0:T(8,128)(2,1)S(1)}, bf16[256,256]{1,0:T(8,128)(2,1)S(1)}, u32[]{:S(2)}, u32[]{:S(2)}) collective-permute-start(bf16[256,256]{1,0:T(8,128)(2,1)S(1)} %get-tuple-element.16.tails), channel_id=1, source_target_pairs={{0,32},{32,64},{64,96},{96,128},{128,160},{160,192},{192,224},{256... | collective-permute-start | bytes 393224 | tf_op jit(solution)/shard_map/ppermute | solution.py:306
  5.3 3.3 %collective-permute-start = (bf16[256,256]{1,0:T(8,128)(2,1)S(1)}, bf16[256,256]{1,0:T(8,128)(2,1)S(1)}, u32[]{:S(2)}, u32[]{:S(2)}) collective-permute-start(bf16[256,256]{1,0:T(8,128)(2,1)S(1)} %get-tuple-element.16.tails), channel_id=1, source_target_pairs={{224,256},{480,512},{736,768},{225,257},{481,513},{737,769},{226,2... | collective-permute-start | bytes 393224 | tf_op jit(solution)/shard_map/ppermute | solution.py:305
  6.0 2.0 %copy-start = (bf16[256,256]{1,0:T(8,128)(2,1)S(1)}, bf16[256,256]{1,0:T(8,128)(2,1)}, u32[]{:S(2)}) copy-start(bf16[256,256]{1,0:T(8,128)(2,1)} %constant.22.ahead.refs_5_) | copy-start | bytes 393220
  6.0 2.0 %copy-start.1 = (bf16[8,16384]{1,0:T(8,128)(2,1)S(1)}, bf16[8,16384]{1,0:T(8,128)(2,1)}, u32[]{:S(2)}) copy-start(bf16[8,16384]{1,0:T(8,128)(2,1)} %taps.5) | copy-start | bytes 786436
  6.0 2.0 %copy-start.3 = (bf16[256,128]{1,0:T(8,128)(2,1)S(1)}, bf16[256,128]{1,0:T(8,128)(2,1)}, u32[]{:S(2)}) copy-start(bf16[256,128]{1,0:T(8,128)(2,1)} %constant.21.outer.refs_3_) | copy-start | bytes 196612
  6.0 2.0 %copy-start.4 = (f32[128,128]{1,0:T(8,128)S(1)}, f32[128,128]{1,0:T(8,128)}, u32[]{:S(2)}) copy-start(f32[128,128]{1,0:T(8,128)} %constant.17.clone.sin.refs_8_) | copy-start | bytes 196612
  6.0 2.0 %copy-start.5 = (f32[128,128]{1,0:T(8,128)S(1)}, f32[128,128]{1,0:T(8,128)}, u32[]{:S(2)}) copy-start(f32[128,128]{1,0:T(8,128)} %constant.16.clone.cos.refs_7_) | copy-start | bytes 196612
  9.1 51.2 %copy-start.6 = (bf16[256,256]{1,0:T(8,128)(2,1)S(1)}, bf16[256,256]{1,0:T(8,128)(2,1)}, u32[]{:S(2)}) copy-start(bf16[256,256]{1,0:T(8,128)(2,1)} %constant.24.refs_6_) | copy-start | bytes 393220
  9.1 51.1 %copy-start.7 = (bf16[128,256]{1,0:T(8,128)(2,1)S(1)}, bf16[128,256]{1,0:T(8,128)(2,1)}, u32[]{:S(2)}) copy-start(bf16[128,256]{1,0:T(8,128)(2,1)} %constant.23.refs_4_) | copy-start | bytes 196612
  9.1 51.1 %copy-start.8 = (f32[256]{0:T(256)S(1)}, f32[256]{0:T(256)}, u32[]{:S(2)}) copy-start(f32[256]{0:T(256)} %refs_2_.1) | copy-start | bytes 3076
  61.6 26.1 %copy-start.2 = (bf16[256,512]{1,0:T(8,128)(2,1)S(1)}, bf16[256,512]{1,0:T(8,128)(2,1)}, u32[]{:S(2)}) copy-start(bf16[256,512]{1,0:T(8,128)(2,1)} %gate.5) | copy-start | bytes 786436

commit v7 on v5

--- a/solution.py
+++ b/solution.py
@@ -10,8 +10,8 @@
 SPLIT = False
 LANES = 128
 ROW = 8
-PARTS = 4
-BATCH = 2
+PARTS = 2
+BATCH = 1
 VMEM = pl.BlockSpec(memory_space=pltpu.VMEM)
 SMEM = pl.BlockSpec(memory_space=pltpu.SMEM)
 BF16 = jnp.bfloat16
@@ -80,13 +80,13 @@
     for copy in copies:
         copy.start()
     copies[0].wait()
-    for g in range(groups // 2):
+    for g in range(groups // 4):
         matrices[g] = band(held, g)
     for copy in copies[1:]:
         copy.wait()
     for g in range(groups):
         at = pl.ds(g * rows, rows)
-        if g >= groups // 2:
+        if g >= groups // 4:
             matrices[g] = band(held, g)
         mixed = (keys[at, :].astype(F32) * values[at, :].astype(F32)).astype(BF16)
         tails[at, :LANES] = mixed[:, LANES:]

time: 88.9 us -> 88.9 us (level)
  the two profiles are of different devices: /device:TPU:121 before, /device:TPU:113 now
where the time goes in v7:
time: 88.9 us; the launch traced here: 88.6 us
  blocking collectives  77.2 us (87%)
  Pallas kernels  6.8 us (8%)
  starting transfers between devices  4.35 us (5%)
    all_to_all x2, blocking collectives, swap(): return lax.all_to_all(data, 'ctx', split_axis=0, concat_axis=0, tiled=True)  77.2 us
    pallas_call x5, Pallas kernels, call(): pl.pallas_call(kernel, out_shape=outs, grid=(1,), in_specs=specs or [VMEM...  6.05 us
    ppermute x1, starting transfers between devices, shards(): close = lax.ppermute(tails, 'ctx', [p for p in pairs if p[1] % ROW])  3.68 us
  transfers between devices with their start and end apart: 2, of which 0 were waited for; matrix products, arithmetic and copies ran while one was open for 0% of the time, Pallas kernels for 3%

profile of v7, /device:TPU:113, one launch (start us, length us, event | category | flops | bytes accessed | tf_op | source)
XLA Modules:
  0.0 88.6 jit_solution(3491176300665186854)
XLA Ops:
  0.0 1.6 %shard_map.145 = (bf16[256,256]{1,0:T(8,128)(2,1)S(1)}, bf16[16,256,128]{2,1,0:T(8,128)(2,1)S(1)}) custom-call(bf16[256,512]{1,0:T(8,128)(2,1)} %value.3, bf16[256,512]{1,0:T(8,128)(2,1)} %key.3, bf16[256,512]{1,0:T(8,128)(2,1)} %gate_one.1, bf16[16,128]{1,0:T(8,128)(2,1)} %taps.3), custom_call_target="tpu_custom_call" | custom-call | tf_op jit(solution)/shard_map/pallas_call | solution.py:30
  1.6 3.7 %collective-permute-start.1 = (bf16[256,256]{1,0:T(8,128)(2,1)S(1)}, bf16[256,256]{1,0:T(8,128)(2,1)S(1)}, u32[]{:S(2)}, u32[]{:S(2)}) collective-permute-start(bf16[256,256]{1,0:T(8,128)(2,1)S(1)} %get-tuple-element.16.tails), channel_id=1, source_target_pairs={{0,32},{32,64},{64,96},{96,128},{128,160},{160,192},{192,224},{256... | collective-permute-start | bytes 393224 | tf_op jit(solution)/shard_map/ppermute | solution.py:300
  5.3 0.7 collective-permute-start
  6.0 0.0 copy-start
  6.0 0.0 copy-start.1
  6.0 0.0 copy-start.3
  6.0 0.0 copy-start.4
  6.0 0.0 copy-start.5
  6.1 2.0 %shard_map.146 = (bf16[256,128]{1,0:T(8,128)(2,1)S(1)}, bf16[256,256]{1,0:T(8,128)(2,1)S(1)}, bf16[16,256,128]{2,1,0:T(8,128)(2,1)S(1)}, bf16[256,128]{1,0:T(8,1...) custom-call(bf16[256,512]{1,0:T(8,128)(2,1)} %value.3, bf16[256,512]{1,0:T(8,128)(2,1)} %key.3, ...), custom_call_target="tpu_custom_call" | custom-call | tf_op jit(solution)/shard_map/pallas_call | solution.py:30
  8.0 0.0 copy-done
  8.0 0.0 copy-done.1
  8.1 0.0 copy-done.3
  8.1 0.0 copy-done.4
  8.1 0.0 copy-done.5
  8.1 0.5 shard_map.147.refs_1_
  8.6 0.0 collective-permute-done.1.close
  8.7 0.0 collective-permute-done.far
  8.7 0.5 shard_map.148
  9.2 0.0 copy-start.6
  9.2 0.0 copy-start.7
  9.2 0.0 copy-start.8
  9.2 51.1 %all_to_all.10.refs_0_ = bf16[32,8,512]{2,1,0:T(8,128)(2,1)S(1)} all-to-all(bf16[32,8,512]{2,1,0:T(8,128)(2,1)S(1)} %bitcast.2), channel_id=1, replica_groups=mesh['ctx'=32,'ch'=32] {'ctx'}, dimensions={0} | all-to-all | bytes 524288 | tf_op jit(solution)/shard_map/all_to_all | solution.py:343
  60.3 0.0 copy-done.6
  60.3 0.0 copy-done.7
  60.3 0.0 copy-done.8
  60.3 1.4 %shard_map.149 = bf16[32,8,512]{2,1,0:T(8,128)(2,1)S(1)} custom-call(bf16[32,8,512]{2,1,0:T(8,128)(2,1)S(1)} %all_to_all.10.refs_0_, f32[8,128,256]{2,1,0:T(8,128)S(1)} %shard_map.147.refs_1_, f32[256]{0:T(256)S(1)} %copy-done.8, bf16[256,128]{1,0:T(8,128)(2,1)S(1)} %copy-done.3, bf16[128,256]{1,0:T(8,128)(2,1)S(1)} %copy-done.7, ...), custom_call_target="tpu_custom_call" | custom-call | tf_op jit(solution)/shard_map/pallas_call | solution.py:30
  61.8 0.0 copy-start.2
  61.8 26.1 %all_to_all.11 = bf16[32,8,512]{2,1,0:T(8,128)(2,1)S(1)} all-to-all(bf16[32,8,512]{2,1,0:T(8,128)(2,1)S(1)} %shard_map.149), channel_id=1, replica_groups=mesh['ctx'=32,'ch'=32] {'ctx'}, dimensions={0} | all-to-all | bytes 524288 | tf_op jit(solution)/shard_map/all_to_all | solution.py:343
  87.9 0.0 copy-done.2
  87.9 0.7 gate.4
Async XLA Ops:
  1.6 7.0 %collective-permute-start.1 = (bf16[256,256]{1,0:T(8,128)(2,1)S(1)}, bf16[256,256]{1,0:T(8,128)(2,1)S(1)}, u32[]{:S(2)}, u32[]{:S(2)}) collective-permute-start(bf16[256,256]{1,0:T(8,128)(2,1)S(1)} %get-tuple-element.16.tails), channel_id=1, source_target_pairs={{0,32},{32,64},{64,96},{96,128},{128,160},{160,192},{192,224},{256... | collective-permute-start | bytes 393224 | tf_op jit(solution)/shard_map/ppermute | solution.py:300
  5.3 3.3 %collective-permute-start = (bf16[256,256]{1,0:T(8,128)(2,1)S(1)}, bf16[256,256]{1,0:T(8,128)(2,1)S(1)}, u32[]{:S(2)}, u32[]{:S(2)}) collective-permute-start(bf16[256,256]{1,0:T(8,128)(2,1)S(1)} %get-tuple-element.16.tails), channel_id=1, source_target_pairs={{224,256},{480,512},{736,768},{225,257},{481,513},{737,769},{226,2... | collective-permute-start | bytes 393224 | tf_op jit(solution)/shard_map/ppermute | solution.py:299
  6.0 2.0 %copy-start = (bf16[256,256]{1,0:T(8,128)(2,1)S(1)}, bf16[256,256]{1,0:T(8,128)(2,1)}, u32[]{:S(2)}) copy-start(bf16[256,256]{1,0:T(8,128)(2,1)} %constant.22.ahead.refs_5_) | copy-start | bytes 393220
  6.0 2.0 %copy-start.1 = (bf16[8,16384]{1,0:T(8,128)(2,1)S(1)}, bf16[8,16384]{1,0:T(8,128)(2,1)}, u32[]{:S(2)}) copy-start(bf16[8,16384]{1,0:T(8,128)(2,1)} %taps.5) | copy-start | bytes 786436
  6.0 2.0 %copy-start.3 = (bf16[256,128]{1,0:T(8,128)(2,1)S(1)}, bf16[256,128]{1,0:T(8,128)(2,1)}, u32[]{:S(2)}) copy-start(bf16[256,128]{1,0:T(8,128)(2,1)} %constant.21.outer.refs_3_) | copy-start | bytes 196612
  6.0 2.0 %copy-start.4 = (f32[128,128]{1,0:T(8,128)S(1)}, f32[128,128]{1,0:T(8,128)}, u32[]{:S(2)}) copy-start(f32[128,128]{1,0:T(8,128)} %constant.17.clone.sin.refs_8_) | copy-start | bytes 196612
  6.0 2.0 %copy-start.5 = (f32[128,128]{1,0:T(8,128)S(1)}, f32[128,128]{1,0:T(8,128)}, u32[]{:S(2)}) copy-start(f32[128,128]{1,0:T(8,128)} %constant.16.clone.cos.refs_7_) | copy-start | bytes 196612
  9.2 51.2 %copy-start.6 = (bf16[256,256]{1,0:T(8,128)(2,1)S(1)}, bf16[256,256]{1,0:T(8,128)(2,1)}, u32[]{:S(2)}) copy-start(bf16[256,256]{1,0:T(8,128)(2,1)} %constant.24.refs_6_) | copy-start | bytes 393220
  9.2 51.1 %copy-start.7 = (bf16[128,256]{1,0:T(8,128)(2,1)S(1)}, bf16[128,256]{1,0:T(8,128)(2,1)}, u32[]{:S(2)}) copy-start(bf16[128,256]{1,0:T(8,128)(2,1)} %constant.23.refs_4_) | copy-start | bytes 196612
  9.2 51.1 %copy-start.8 = (f32[256]{0:T(256)S(1)}, f32[256]{0:T(256)}, u32[]{:S(2)}) copy-start(f32[256]{0:T(256)} %refs_2_.1) | copy-start | bytes 3076
  61.8 26.1 %copy-start.2 = (bf16[256,512]{1,0:T(8,128)(2,1)S(1)}, bf16[256,512]{1,0:T(8,128)(2,1)}, u32[]{:S(2)}) copy-start(bf16[256,512]{1,0:T(8,128)(2,1)} %gate.5) | copy-start | bytes 786436
